TPU v7x, 256 devices: a whole 4x4x8 slice. The times are simulated.
256 devices in a mesh: row: 8 (over z), col: 16 (over x, y), grid: 2 (over core).
Axes of the slice: x: 4, y: 4, z: 8, core: 2. Of those that a mesh axis runs over, the one named last changes fastest.
Arguments:
- density: bfloat16 [2, 8, 4, 128, 2048], P(None, 'row', None, 'grid', 'col'), may hold values from -0.01171875 to 0.01171875
- basis_values: bfloat16 [128, 256, 512], P(('row', 'col'), 'grid'), may hold values from -6 to 6
- quad_weight: float32 [128, 256], P(('row', 'col'), 'grid'), may hold values from 0.01 to 0.1
- screen: int32 [128, 256], P(('row', 'col'), 'grid'), may hold values 0 or 1
- tile_list: int32 [128, 4], replicated, may hold values from 0 to 15, as said below
Outputs:
- potential_first: bfloat16 [2, 8, 4, 128, 2048], P(None, 'row', None, 'grid', 'col')
- potential_second: bfloat16 [2, 8, 4, 128, 2048], P(None, 'row', None, 'grid', 'col')
Inputs may be any that keep to these rules, and one draw needn't show every extreme that they name: `tile_list`: the 4 tile indices of a batch have distinct remainders modulo 8.
All inputs are finite; a program needn't handle non-finite values. No bound on the sum of `screen` on one device may be relied on, other than what follows from the above.
Results may differ from a plain program's by a relative error of at most 0.014.
Values may be sent and summed in bfloat16 or wider, within the bound.
No kernel may reach another device: no remote copies, remote signals or barrier semaphores. Data moves between devices by JAX's collectives and lax.ppermute only.
A program may use at most 64 MiB of HBM per device.

v0:
```python
import jax
import jax.numpy as jnp
from jax import lax
from jax.sharding import PartitionSpec as P

MIXING = 0.001


def from_everyone(x, axis):
    copies = jnp.broadcast_to(x, (lax.axis_size(axis), *x.shape))
    return lax.all_to_all(copies, axis, split_axis=0, concat_axis=0, tiled=True)


def laid_out(tiles, dim):
    tiles = jnp.moveaxis(tiles, 0, dim)
    lengths = tiles.shape
    return tiles.reshape(*lengths[:dim], lengths[dim] * lengths[dim + 1], *lengths[dim + 2 :])


def gather_directly(x, axis, dim):
    tiles = from_everyone(x, axis)
    return laid_out(tiles, dim)


def split_up(x, dim, length):
    before, after = (x.shape[:dim], x.shape[dim + 1 :])
    return jnp.moveaxis(x.reshape(*before, length, -1, *after), dim, 0)


def sum_at_owner(x, axis, dim):
    length = lax.axis_size(axis)
    tiles = lax.all_to_all(split_up(x, dim, length), axis, 0, 0, tiled=True)
    return jnp.sum(tiles.astype(jnp.float32), axis=0)


def local_potential(densities):
    total_density = densities[:, 0:1]
    spin_density = densities[:, 1:4]
    first_part = total_density / jnp.sqrt(1.0 + total_density * total_density)
    spin_norm = jnp.sqrt(1.0 + jnp.sum(spin_density * spin_density, axis=1, keepdims=True))
    return jnp.concatenate([first_part, spin_density / spin_norm], axis=1)


def build(density, basis_values, point_weight, tile_list):
    n_row = lax.axis_size("row")
    n_col = lax.axis_size("col")
    n_grid = lax.axis_size("grid")
    my_row = lax.axis_index("row")
    my_col = lax.axis_index("col")
    per_batch = tile_list.shape[1]
    row_tiles = density.shape[0]
    components = density.shape[2]
    half_tile = density.shape[3]
    tile_width = half_tile * n_grid
    span = per_batch * tile_width
    strip = gather_directly(density, "col", 4)
    n_tiles = strip.shape[4] // tile_width
    tile_blocks = strip.reshape(row_tiles, components, half_tile, n_tiles, tile_width)
    peer_lists = lax.dynamic_index_in_dim(
        tile_list.reshape(n_row, n_col, per_batch), my_col, axis=1, keepdims=False
    )
    matches = peer_lists % n_row == my_row
    present = jnp.any(matches, axis=1)
    peer_multiple = jnp.sum(jnp.where(matches, peer_lists // n_row, 0), axis=1)

    def pack(multiple, columns):
        row_block = lax.dynamic_index_in_dim(tile_blocks, multiple, 0, keepdims=False)
        return jnp.take(row_block, columns, axis=2)

    payload = jax.vmap(pack)(peer_multiple, peer_lists).reshape(n_row, components, half_tile, span)
    own_list = lax.dynamic_index_in_dim(peer_lists, my_row, 0, keepdims=False)
    residue = own_list % n_row
    arrived = lax.all_to_all(payload, "row", split_axis=0, concat_axis=0, tiled=True)
    own_half = jnp.take(arrived, residue, axis=0)
    gathered_rows = gather_directly(own_half, "grid", 2)
    blocks = [gathered_rows[:, comp].reshape(span, span) for comp in range(components)]
    samples = basis_values[0]
    samples_wide = samples.astype(jnp.float32)
    densities = jnp.stack(
        [
            jnp.sum(
                jnp.dot(samples, blocks[comp], preferred_element_type=jnp.float32) * samples_wide,
                axis=1,
            )
            for comp in range(components)
        ],
        axis=1,
    )
    potential_scale = point_weight[:, None] * local_potential(densities)
    slabs = []
    for comp in range(components):
        weighted = (samples_wide * potential_scale[:, comp : comp + 1]).astype(jnp.bfloat16)
        partial_value = lax.dot_general(
            samples, weighted, (((0,), (0,)), ((), ())), preferred_element_type=jnp.float32
        )
        slabs.append(partial_value.astype(jnp.bfloat16).reshape(per_batch, n_grid, half_tile, span))
    rounded = jnp.stack(slabs, axis=2)
    pick_multiple = present[:, None] & (peer_multiple[:, None] == jnp.arange(row_tiles)[None, :])
    pick_columns = peer_lists[:, :, None] == jnp.arange(n_tiles)[None, None, :]
    placing = (pick_multiple[:, :, None, None] & pick_columns[:, None, :, :]).astype(jnp.bfloat16)
    terms = lax.optimization_barrier(rounded).astype(jnp.float32)
    halves = sum_at_owner(terms.astype(jnp.bfloat16), "grid", 1)
    halves = halves.reshape(per_batch, components, half_tile, span)
    outgoing = jnp.zeros((n_row, components, half_tile, span), jnp.float32).at[residue].set(halves)
    incoming = lax.all_to_all(
        outgoing.astype(jnp.bfloat16), "row", split_axis=0, concat_axis=0, tiled=True
    ).astype(outgoing.dtype)
    incoming = incoming.reshape(n_row, components, half_tile, per_batch, tile_width)
    upper = incoming.astype(jnp.bfloat16)
    lower = (incoming - upper.astype(jnp.float32)).astype(jnp.bfloat16)
    summed = jnp.einsum("qkst,qcasb->kcatb", placing, upper, preferred_element_type=jnp.float32)
    summed = summed + jnp.einsum(
        "qkst,qcasb->kcatb", placing, lower, preferred_element_type=jnp.float32
    )
    summed = summed.reshape(row_tiles, components, half_tile, n_tiles * tile_width)
    owned = sum_at_owner(summed.astype(jnp.bfloat16), "col", 3)
    return owned.astype(jnp.bfloat16)[:, None]


def body(density, basis_values, quad_weight, screen, tile_list):
    point_weight = quad_weight[0] * screen[0].astype(jnp.float32)
    potential_first = build(density, basis_values, point_weight, tile_list)
    updated = (density.astype(jnp.float32) + MIXING * potential_first.astype(jnp.float32)).astype(
        jnp.bfloat16
    )
    potential_second = build(updated, basis_values, point_weight, tile_list)
    return (potential_first, potential_second)


def solution(mesh):
    in_specs = (
        P(None, "row", None, "grid", "col"),
        P(("row", "col"), "grid", None),
        P(("row", "col"), "grid"),
        P(("row", "col"), "grid"),
        P(),
    )
    out_specs = (P(None, "row", None, "grid", "col"), P(None, "row", None, "grid", "col"))
    return jax.shard_map(body, mesh=mesh, in_specs=in_specs, out_specs=out_specs, check_vma=False)
```

profile of v0, /device:TPU:1, one launch (start us, length us, event | category | flops | bytes accessed | tf_op | source)
XLA Modules:
  0.0 466.3 jit_solution(16413118977743419377)
XLA Ops:
  0.6 2.7 broadcast_in_dim.36
  3.4 7.8 %all-to-all-start = ((bf16[16,2,1,4,64,128]{5,4,3,1,2,0:T(8,128)(2,1)}), bf16[16,2,1,4,64,128]{5,4,3,1,2,0:T(8,128)(2,1)}, u32[]{:S(2)}, u32[]{:S(2)}) async-start(bf16[16,2,1,4,64,128]{5,4,3,1,2,0:T(8,128)(2,1)} %broadcast_in_dim.36), calls=%async_computation | async-start | bytes 4194304 | tf_op jit(solution)/shard_map/all_to_all | solution.py:11
  11.7 27.3 %all-to-all-done = bf16[16,2,1,4,64,128]{5,4,3,1,2,0:T(8,128)(2,1)} async-done(((bf16[16,2,1,4,64,128]{5,4,3,1,2,0:T(8,128)(2,1)}), bf16[16,2,1,4,64,128]{5,4,3,1,2,0:T(8,128)(2,1)}, u32[]{:S(2)}, u32[]{:S(2)}) %all-to-all-start) | async-done | bytes 2097184 | tf_op jit(solution)/shard_map/all_to_all | solution.py:11
  39.1 1.8 copy.148
  40.9 4.6 gather_fusion
  45.5 4.3 gather_fusion.2
  49.9 3.1 fusion.11
  53.0 4.1 reshape.319
  57.1 8.2 %all-to-all-start.1 = ((bf16[8,4,64,512]{3,2,1,0:T(8,128)(2,1)}), bf16[8,4,64,512]{3,2,1,0:T(8,128)(2,1)S(1)}, u32[]{:S(2)}, u32[]{:S(2)}) async-start(bf16[8,4,64,512]{3,2,1,0:T(8,128)(2,1)} %reshape.319), calls=%async_computation.1 | async-start | bytes 4194304 | tf_op jit(solution)/shard_map/all_to_all | solution.py:73
  65.8 47.8 %all-to-all-done.1 = bf16[8,4,64,512]{3,2,1,0:T(8,128)(2,1)S(1)} async-done(((bf16[8,4,64,512]{3,2,1,0:T(8,128)(2,1)}), bf16[8,4,64,512]{3,2,1,0:T(8,128)(2,1)S(1)}, u32[]{:S(2)}, u32[]{:S(2)}) %all-to-all-start.1) | async-done | bytes 2097184 | tf_op jit(solution)/shard_map/all_to_all | solution.py:73
  113.6 0.6 gather_fusion.3
  114.6 9.0 %all_to_all.60 = bf16[2,4,4,64,512]{4,3,2,1,0:T(8,128)(2,1)S(1)} all-to-all(bf16[2,4,4,64,512]{4,3,2,1,0:T(8,128)(2,1)S(1)} %broadcast_in_dim.37), channel_id=1, replica_groups=mesh['row'=8,'col'=16,'grid'=2] {'grid'}, dimensions={0} | all-to-all | bytes 4194304 | tf_op jit(solution)/shard_map/all_to_all | solution.py:11
  124.0 0.4 fusion.27
  124.4 0.4 fusion.28
  124.7 0.4 fusion.29
  125.2 0.4 fusion.26
  125.6 0.4 convolution_convert_fusion.7
  125.9 0.4 convolution_convert_fusion.6
  126.3 0.4 convolution_convert_fusion.5
  126.7 0.4 convolution_convert_fusion.4
  127.5 5.4 %all_to_all.61 = bf16[2,4,1,4,64,512]{5,4,1,3,2,0:T(8,128)(2,1)S(1)} all-to-all(bf16[2,4,1,4,64,512]{5,4,1,3,2,0:T(8,128)(2,1)S(1)} %bitcast.334), channel_id=1, replica_groups=mesh['row'=8,'col'=16,'grid'=2] {'grid'}, dimensions={0} | all-to-all | bytes 4194304 | tf_op jit(solution)/shard_map/all_to_all | solution.py:32
  132.9 0.4 convert_reduce_fusion.1
  133.5 2.5 broadcast.210.clone
  136.0 3.5 scatter_fusion
  139.5 3.8 convert_element_type.207
  143.3 4.5 all-to-all-start.4
  148.0 48.1 %all-to-all-done.4 = bf16[8,4,64,512]{3,2,1,0:T(8,128)(2,1)} async-done(((bf16[8,4,64,512]{3,2,1,0:T(8,128)(2,1)}), bf16[8,4,64,512]{3,2,1,0:T(8,128)(2,1)}, u32[]{:S(2)}, u32[]{:S(2)}) %all-to-all-start.4) | async-done | bytes 2097184 | tf_op jit(solution)/shard_map/all_to_all | solution.py:105
  196.1 2.5 reshape.322
  198.7 1.4 fusion.8
  200.1 1.8 fusion.12
  201.8 2.3 copy.80
  204.2 30.9 %all_to_all.62 = bf16[16,2,4,64,128]{4,1,3,2,0:T(2,128)(2,1)S(1)} all-to-all(bf16[16,2,4,64,128]{4,1,3,2,0:T(2,128)(2,1)S(1)} %copy.80), channel_id=1, replica_groups=mesh['row'=8,'col'=16,'grid'=2] {'col'}, dimensions={0} | all-to-all | bytes 4194304 | tf_op jit(solution)/shard_map/all_to_all | solution.py:32
  235.1 2.3 reduce_sum.160
  237.6 0.5 broadcast_in_dim.39
  238.2 29.9 %all_to_all.63 = bf16[16,2,1,4,64,128]{5,4,3,1,2,0:T(8,128)(2,1)S(1)} all-to-all(bf16[16,2,1,4,64,128]{5,4,3,1,2,0:T(8,128)(2,1)S(1)} %broadcast_in_dim.39), channel_id=1, replica_groups=mesh['row'=8,'col'=16,'grid'=2] {'col'}, dimensions={0} | all-to-all | bytes 4194304 | tf_op jit(solution)/shard_map/all_to_all | solution.py:11
  268.2 4.6 gather_fusion.1
  272.8 4.3 gather_fusion.4
  277.2 3.1 fusion.10
  280.3 2.7 reshape.324
  283.1 51.5 %all_to_all.64 = bf16[8,4,64,512]{3,2,1,0:T(8,128)(2,1)} all-to-all(bf16[8,4,64,512]{3,2,1,0:T(8,128)(2,1)S(1)} %reshape.324), channel_id=1, replica_groups=mesh['row'=8,'col'=16,'grid'=2] {'row'}, dimensions={0} | all-to-all | bytes 4194304 | tf_op jit(solution)/shard_map/all_to_all | solution.py:73
  334.6 2.2 gather_fusion.5
  337.2 10.6 %all_to_all.65 = bf16[2,4,4,64,512]{4,3,2,1,0:T(8,128)(2,1)S(1)} all-to-all(bf16[2,4,4,64,512]{4,3,2,1,0:T(8,128)(2,1)S(1)} %broadcast_in_dim.40), channel_id=1, replica_groups=mesh['row'=8,'col'=16,'grid'=2] {'grid'}, dimensions={0} | all-to-all | bytes 4194304 | tf_op jit(solution)/shard_map/all_to_all | solution.py:11
  348.2 0.4 fusion.31
  348.5 0.4 fusion.32
  348.9 0.4 fusion.33
  349.3 0.4 fusion.30
  349.7 0.4 convolution_convert_fusion.3
  350.1 0.4 convolution_convert_fusion.2
  350.8 0.4 convolution_convert_fusion
  351.7 5.3 %all_to_all.66 = bf16[2,4,1,4,64,512]{5,4,1,3,2,0:T(8,128)(2,1)S(1)} all-to-all(bf16[2,4,1,4,64,512]{5,4,1,3,2,0:T(8,128)(2,1)S(1)} %bitcast.335), channel_id=1, replica_groups=mesh['row'=8,'col'=16,'grid'=2] {'grid'}, dimensions={0} | all-to-all | bytes 4194304 | tf_op jit(solution)/shard_map/all_to_all | solution.py:32
  357.0 0.4 convert_reduce_fusion
  357.6 2.5 broadcast.210
  360.0 3.5 scatter_fusion.1
  363.5 2.5 convert_element_type.232
  366.1 54.8 %all_to_all.67 = bf16[8,4,64,512]{3,2,1,0:T(8,128)(2,1)} all-to-all(bf16[8,4,64,512]{3,2,1,0:T(8,128)(2,1)S(1)} %convert_element_type.232), channel_id=1, replica_groups=mesh['row'=8,'col'=16,'grid'=2] {'row'}, dimensions={0} | all-to-all | bytes 4194304 | tf_op jit(solution)/shard_map/all_to_all | solution.py:105
  420.9 2.5 reshape.327
  423.4 1.4 fusion.5
  424.8 1.8 fusion.15
  426.6 3.7 copy.97
  430.3 3.7 all-to-all-start.11
  434.0 0.7 copy.99
  434.7 28.7 %all-to-all-done.11 = bf16[16,2,4,64,128]{4,1,3,2,0:T(2,128)(2,1)S(1)} async-done(((bf16[16,2,4,64,128]{4,1,3,2,0:T(2,128)(2,1)}), bf16[16,2,4,64,128]{4,1,3,2,0:T(2,128)(2,1)S(1)}, u32[]{:S(2)}, u32[]{:S(2)}) %all-to-all-start.11) | async-done | bytes 2097184 | tf_op jit(solution)/shard_map/all_to_all | solution.py:32
  463.3 2.3 reduce_sum.168
  465.6 0.7 copy.100
  (60 shorter events, 4.9 us)
Async XLA Ops:
  3.4 7.8 %copy-start.2 = (s32[128,4]{0,1:T(4,128)S(1)}, s32[128,4]{0,1:T(4,128)}, u32[]{:S(2)}) copy-start(s32[128,4]{0,1:T(4,128)} %param.13) | copy-start | bytes 6148
  3.4 35.7 %all-to-all-start = ((bf16[16,2,1,4,64,128]{5,4,3,1,2,0:T(8,128)(2,1)}), bf16[16,2,1,4,64,128]{5,4,3,1,2,0:T(8,128)(2,1)}, u32[]{:S(2)}, u32[]{:S(2)}) async-start(bf16[16,2,1,4,64,128]{5,4,3,1,2,0:T(8,128)(2,1)} %broadcast_in_dim.36), calls=%async_computation | async-start | bytes 4194304 | tf_op jit(solution)/shard_map/all_to_all | solution.py:11
  57.1 8.4 %copy-start = (bf16[1,128,512]{2,1,0:T(8,128)(2,1)S(1)}, bf16[1,128,512]{2,1,0:T(8,128)(2,1)}, u32[]{:S(2)}) copy-start(bf16[1,128,512]{2,1,0:T(8,128)(2,1)} %param.10) | copy-start | bytes 393220
  57.1 8.6 %copy-start.3 = (f32[1,128]{1,0:T(1,128)S(1)}, f32[1,128]{1,0:T(1,128)}, u32[]{:S(2)}) copy-start(f32[1,128]{1,0:T(1,128)} %param.11) | copy-start | bytes 1540
  57.1 8.6 %copy-start.4 = (s32[1,128]{1,0:T(1,128)S(1)}, s32[1,128]{1,0:T(1,128)}, u32[]{:S(2)}) copy-start(s32[1,128]{1,0:T(1,128)} %param.12) | copy-start | bytes 1540
  57.1 56.4 %all-to-all-start.1 = ((bf16[8,4,64,512]{3,2,1,0:T(8,128)(2,1)}), bf16[8,4,64,512]{3,2,1,0:T(8,128)(2,1)S(1)}, u32[]{:S(2)}, u32[]{:S(2)}) async-start(bf16[8,4,64,512]{3,2,1,0:T(8,128)(2,1)} %reshape.319), calls=%async_computation.1 | async-start | bytes 4194304 | tf_op jit(solution)/shard_map/all_to_all | solution.py:73
  143.3 52.8 %all-to-all-start.4 = ((bf16[8,4,64,512]{3,2,1,0:T(8,128)(2,1)}), bf16[8,4,64,512]{3,2,1,0:T(8,128)(2,1)}, u32[]{:S(2)}, u32[]{:S(2)}) async-start(bf16[8,4,64,512]{3,2,1,0:T(8,128)(2,1)} %convert_element_type.207), calls=%async_computation.4 | async-start | bytes 4194304 | tf_op jit(solution)/shard_map/all_to_all | solution.py:105
  235.1 2.3 copy-start.1
  430.3 33.1 %all-to-all-start.11 = ((bf16[16,2,4,64,128]{4,1,3,2,0:T(2,128)(2,1)}), bf16[16,2,4,64,128]{4,1,3,2,0:T(2,128)(2,1)S(1)}, u32[]{:S(2)}, u32[]{:S(2)}) async-start(bf16[16,2,4,64,128]{4,1,3,2,0:T(2,128)(2,1)} %copy.97), calls=%async_computation.11 | async-start | bytes 4194304 | tf_op jit(solution)/shard_map/all_to_all | solution.py:32
where the time goes:
time: 467 us; the launch traced here: 466 us
  blocking collectives  197 us (42%)
  waiting for transfers between devices  152 us (33%)
  local copies, waits for them, and re-layouts  60.1 us (13%)
  starting transfers between devices  24.3 us (5%)
  other arithmetic  19.3 us (4%)
  matrix products  12.1 us (3%)
    all_to_all x1, blocking collectives, build(): lax.all_to_all(outgoing.astype(jnp.bfloat16), 'row', split_axis=0, concat...  54.8 us
    all_to_all x1, blocking collectives, build(): lax.all_to_all(payload, 'row', split_axis=0, concat_axis=0, tiled=True)  51.5 us
    all_to_all x3, blocking collectives, from_everyone(): return lax.all_to_all(copies, axis, split_axis=0, concat_axis=0, tiled=True)  49.4 us
    all_to_all x1, waiting for transfers between devices, build(): lax.all_to_all(outgoing.astype(jnp.bfloat16), 'row', split_axis=0, concat...  48.1 us
    all_to_all x1, waiting for transfers between devices, build(): lax.all_to_all(payload, 'row', split_axis=0, concat_axis=0, tiled=True)  47.8 us
    all_to_all x3, blocking collectives, sum_at_owner(): tiles = lax.all_to_all(split_up(x, dim, length), axis, 0, 0, tiled=True)  41.7 us
    all_to_all x1, waiting for transfers between devices, sum_at_owner(): tiles = lax.all_to_all(split_up(x, dim, length), axis, 0, 0, tiled=True)  28.7 us
    all_to_all x1, waiting for transfers between devices, from_everyone(): return lax.all_to_all(copies, axis, split_axis=0, concat_axis=0, tiled=True)  27.3 us
  transfers between devices with their start and end apart: 4, of which 4 were waited for; matrix products, arithmetic and copies ran while one was open for 0% of the time, Pallas kernels for 0%

commit v1 on v0

v1 whole, which is shorter than its diff:
```python
import functools

import jax
import jax.numpy as jnp
from jax import lax
from jax.experimental import pallas as pl
from jax.experimental.pallas import tpu as pltpu
from jax.sharding import PartitionSpec as P

MIXING = 0.001
VMEM_BYTES = 32 * 1024 * 1024


def everyone(x, n):
    return jnp.broadcast_to(x[None], (n, *x.shape))


def find(tile_list, batch, n_row, my_row):
    columns = [tile_list[batch, s] for s in range(tile_list.shape[1])]
    slot = jnp.int32(0)
    multiple = jnp.int32(0)
    present = jnp.bool_(False)
    for s, tile in enumerate(columns):
        match = lax.rem(tile, n_row) == my_row
        slot = jnp.where(match, s, slot)
        multiple = jnp.where(match, lax.div(tile, n_row), multiple)
        present = jnp.logical_or(present, match)
    return columns, slot, multiple, present


def own_rows(basis, slot, half, tile_width, half_tile):
    points = basis.shape[0] * basis.shape[2]
    block = basis[:, 0, :, pl.ds(pl.multiple_of(slot * tile_width, tile_width), tile_width)]
    block = block.reshape(points, tile_width)
    rows = lax.broadcasted_iota(jnp.int32, (half_tile, tile_width), 0) + half * half_tile
    lanes = lax.broadcasted_iota(jnp.int32, (half_tile, tile_width), 1)
    chosen = jnp.where(rows == lanes, 1.0, 0.0).astype(jnp.bfloat16)
    return lax.dot_general(chosen, block, (((1,), (1,)), ((), ())), preferred_element_type=jnp.float32)


def density_kernel(tile_list, strip, basis, weight, screen, out, block, sums, *, n_row, n_col, comps, half_tile, width):
    step = pl.program_id(0)
    my_row = lax.axis_index("row")
    my_col = lax.axis_index("col")
    half = lax.axis_index("grid")
    span = comps * half_tile
    points = basis.shape[0] * basis.shape[2]

    @pl.when(step == 0)
    def _():
        sums[...] = jnp.zeros_like(sums)
        own = weight[...] * screen[...].astype(jnp.float32)
        sums[comps, 0:1, 0 : own.shape[1]] = own

    columns, slot, multiple, present = find(tile_list, step * n_col + my_col, n_row, my_row)

    @pl.when(present)
    def _():
        for s, tile in enumerate(columns):
            first = pl.multiple_of(multiple * span, span)
            block[:, s * width : (s + 1) * width] = strip[tile, pl.ds(first, span), :]
        samples = basis[:, 0].reshape(points, basis.shape[3])
        part = lax.dot_general(
            block[...], samples, (((1,), (1,)), ((), ())), preferred_element_type=jnp.float32
        )
        rows = own_rows(basis, slot, half, width, half_tile)
        for comp in range(comps):
            piece = part[comp * half_tile : (comp + 1) * half_tile, :] * rows
            sums[comp, pl.ds(step, 1), :] = jnp.sum(piece, axis=0, keepdims=True)

    @pl.when(step == pl.num_programs(0) - 1)
    def _():
        for dest in range(out.shape[0]):
            out[dest] = sums[...]


def potential_kernel(tile_list, arrived, basis, out, scales, acc, *, n_row, n_col, comps, half_tile, width):
    step = pl.program_id(0)
    my_row = lax.axis_index("row")
    my_col = lax.axis_index("col")
    half = lax.axis_index("grid")
    span = comps * half_tile
    points = basis.shape[0] * basis.shape[2]
    n_half = basis.shape[0]
    half_points = basis.shape[2]

    @pl.when(step == 0)
    def _():
        acc[...] = jnp.zeros_like(acc)
        dens = jnp.sum(arrived[:, 0:comps], axis=0)
        total = dens[0]
        spin = [dens[comp] for comp in range(1, comps)]
        norm = jnp.sqrt(1.0 + sum(s * s for s in spin))
        potentials = [total / jnp.sqrt(1.0 + total * total)] + [s / norm for s in spin]
        weights = jnp.concatenate(
            [
                jnp.concatenate(
                    [arrived[q * n_half + h, comps, 0:1, 0:half_points] for h in range(n_half)], axis=1
                )
                for q in range(n_row)
            ],
            axis=0,
        )
        for comp in range(comps):
            scales[comp] = potentials[comp] * weights

    columns, slot, multiple, present = find(tile_list, step * n_col + my_col, n_row, my_row)

    @pl.when(present)
    def _():
        samples = basis[:, 0].reshape(points, basis.shape[3])
        rows = own_rows(basis, slot, half, width, half_tile)
        weighted = jnp.concatenate(
            [(rows * scales[comp, pl.ds(step, 1), :]).astype(jnp.bfloat16) for comp in range(comps)], axis=0
        )
        part = jnp.dot(weighted, samples, preferred_element_type=jnp.float32)
        first = pl.multiple_of(multiple * span, span)
        for s, tile in enumerate(columns):
            acc[tile, pl.ds(first, span), :] += part[:, s * width : (s + 1) * width]

    @pl.when(step == pl.num_programs(0) - 1)
    def _():
        out[...] = acc[...].astype(jnp.bfloat16)


def update_kernel(pieces, density, first, copies):
    total = jnp.sum(pieces[...].astype(jnp.float32), axis=0).astype(jnp.bfloat16)
    first[...] = total
    updated = (density[...].astype(jnp.float32) + MIXING * total.astype(jnp.float32)).astype(jnp.bfloat16)
    for dest in range(copies.shape[0]):
        copies[dest] = updated


def sum_kernel(pieces, out):
    out[...] = jnp.sum(pieces[...].astype(jnp.float32), axis=0).astype(jnp.bfloat16)


def body(density, basis_values, quad_weight, screen, tile_list):
    n_row = lax.axis_size("row")
    n_col = lax.axis_size("col")
    n_grid = lax.axis_size("grid")
    row_tiles, _, comps, half_tile, width = density.shape
    half_points, functions = basis_values.shape[1:]
    points = half_points * n_grid
    rows = row_tiles * comps * half_tile
    span = comps * half_tile
    planes = comps + 1
    sizes = dict(n_row=n_row, n_col=n_col, comps=comps, half_tile=half_tile, width=width)
    own = density.reshape(rows, width)
    basis = lax.all_gather(basis_values, "row", axis=0, tiled=True)
    basis = lax.all_gather(basis, "grid", axis=0, tiled=False)
    params = pltpu.CompilerParams(dimension_semantics=("arbitrary",), vmem_limit_bytes=VMEM_BYTES)
    basis_spec = pl.BlockSpec((n_grid, 1, half_points, functions), lambda b, t: (0, b, 0, 0))
    whole = lambda *shape: pl.BlockSpec(shape, lambda b, t: (0,) * len(shape))
    message = (n_row * n_grid, planes, n_row, points)
    densities = pl.pallas_call(
        functools.partial(density_kernel, **sizes),
        grid_spec=pltpu.PrefetchScalarGridSpec(
            num_scalar_prefetch=1,
            grid=(n_row,),
            in_specs=[whole(n_col, rows, width), basis_spec, whole(1, half_points), whole(1, half_points)],
            out_specs=whole(*message),
            scratch_shapes=[
                pltpu.VMEM((span, functions), jnp.bfloat16),
                pltpu.VMEM((planes, n_row, points), jnp.float32),
            ],
        ),
        out_shape=jax.ShapeDtypeStruct(message, jnp.float32),
        compiler_params=params,
    )
    potentials = pl.pallas_call(
        functools.partial(potential_kernel, **sizes),
        grid_spec=pltpu.PrefetchScalarGridSpec(
            num_scalar_prefetch=1,
            grid=(n_row,),
            in_specs=[whole(*message), basis_spec],
            out_specs=whole(n_col, rows, width),
            scratch_shapes=[
                pltpu.VMEM((comps, n_row, points), jnp.float32),
                pltpu.VMEM((n_col, rows, width), jnp.float32),
            ],
        ),
        out_shape=jax.ShapeDtypeStruct((n_col, rows, width), jnp.bfloat16),
        compiler_params=params,
    )
    chunk = rows // 4
    pieces_spec = pl.BlockSpec((n_col, chunk, width), lambda i: (0, i, 0))
    row_spec = pl.BlockSpec((chunk, width), lambda i: (i, 0))
    owned = jax.ShapeDtypeStruct((rows, width), jnp.bfloat16)
    update = pl.pallas_call(
        update_kernel,
        grid=(rows // chunk,),
        in_specs=[pieces_spec, row_spec],
        out_specs=[row_spec, pieces_spec],
        out_shape=[owned, jax.ShapeDtypeStruct((n_col, rows, width), jnp.bfloat16)],
        compiler_params=params,
    )
    add_up = pl.pallas_call(
        sum_kernel,
        grid=(rows // chunk,),
        in_specs=[pieces_spec],
        out_specs=row_spec,
        out_shape=owned,
        compiler_params=params,
    )

    def build(copies):
        strip = lax.all_to_all(copies, "col", 0, 0, tiled=True)
        partials = densities(tile_list, strip, basis, quad_weight, screen)
        arrived = lax.all_to_all(partials, ("row", "grid"), 0, 0, tiled=True)
        slabs = potentials(tile_list, arrived, basis)
        return lax.all_to_all(slabs, "col", 0, 0, tiled=True)

    first, copies = update(build(everyone(own, n_col)), own)
    second = add_up(build(copies))
    shape = density.shape
    return first.reshape(shape), second.reshape(shape)


def solution(mesh):
    in_specs = (
        P(None, "row", None, "grid", "col"),
        P(("row", "col"), "grid", None),
        P(("row", "col"), "grid"),
        P(("row", "col"), "grid"),
        P(),
    )
    out_specs = (P(None, "row", None, "grid", "col"), P(None, "row", None, "grid", "col"))
    return jax.shard_map(body, mesh=mesh, in_specs=in_specs, out_specs=out_specs, check_vma=False)
```

time: 467 us -> 260 us (0.56)
  waiting for transfers between devices: 152 us -> 62.7 us
  local copies, waits for them, and re-layouts: 60.1 us -> 4.36 us
  blocking collectives: 197 us -> 154 us
  other arithmetic: 19.3 us -> 0 us
  starting transfers between devices: 24.3 us -> 6.73 us
  Pallas kernels: 0 us -> 17.3 us
  between operations: 1.11 us -> 14.1 us
  matrix products: 12.1 us -> 0 us
    all_to_all x4 -> x1, waiting for transfers between devices: 152 us -> 22.7 us  [build(): strip = lax.all_to_all(copies, 'col', 0, 0, tiled=True)]
    all_to_all x8 -> x5, blocking collectives: 197 us -> 154 us  [the longest x2 65.8 us: build(): return lax.all_to_all(slabs, 'col', 0, 0, tiled=True)]
    all_gather x0 -> x2, waiting for transfers between devices: none -> 39.3 us  [the longest x1 39.3 us: body(): basis = lax.all_gather(basis_values, 'row', axis=0, tiled=True)]
    gather x8 -> x0, local copies, waits for them, and re-layouts: 20.9 us -> none  [the longest x2 9.27 us: pack(): lax.dynamic_index_in_dim(tile_blocks, multiple, 0, keepdims=False)]
    all_to_all x4 -> x1, starting transfers between devices: 24.3 us -> 6.66 us  [build(): strip = lax.all_to_all(copies, 'col', 0, 0, tiled=True)]
    pallas_call x0 -> x6, Pallas kernels: none -> 17.3 us  [the longest x2 7.74 us: build(): slabs = potentials(tile_list, arrived, basis)]
    dot_general x20 -> x0, matrix products: 12.1 us -> none  [the longest x2 3.55 us: build(): jnp.einsum('qkst,qcasb->kcatb', placing, lower, preferred_element_type=jn...]
    reshape x5 -> x0, local copies, waits for them, and re-layouts: 12 us -> none  [the longest x2 6.87 us: build(): jax.vmap(pack)(peer_multiple, peer_lists)]
  transfers between devices with their start and end apart: 4 -> 3, of which waited for: 4 -> 2; matrix products, arithmetic and copies ran while one was open for 0% -> 1% of each run, Pallas kernels for 0% -> 0%
where the time goes in v1:
time: 260 us; the launch traced here: 259 us
  blocking collectives  154 us (59%)
  waiting for transfers between devices  62.7 us (24%)
  Pallas kernels  17.3 us (7%)
  between operations  14.1 us (5%)
  starting transfers between devices  6.73 us (3%)
  local copies, waits for them, and re-layouts  4.36 us (2%)
    all_to_all x2, blocking collectives, build(): return lax.all_to_all(slabs, 'col', 0, 0, tiled=True)  65.8 us
    all_to_all x2, blocking collectives, build(): arrived = lax.all_to_all(partials, ('row', 'grid'), 0, 0, tiled=True)  58.2 us
    all_gather x1, waiting for transfers between devices, body(): basis = lax.all_gather(basis_values, 'row', axis=0, tiled=True)  39.3 us
    all_to_all x1, blocking collectives, build(): strip = lax.all_to_all(copies, 'col', 0, 0, tiled=True)  29.7 us
    all_to_all x1, waiting for transfers between devices, build(): strip = lax.all_to_all(copies, 'col', 0, 0, tiled=True)  22.7 us
    pallas_call x2, Pallas kernels, build(): slabs = potentials(tile_list, arrived, basis)  7.74 us
    all_to_all x1, starting transfers between devices, build(): strip = lax.all_to_all(copies, 'col', 0, 0, tiled=True)  6.66 us
    pallas_call x2, Pallas kernels, build(): partials = densities(tile_list, strip, basis, quad_weight, screen)  6.24 us
  transfers between devices with their start and end apart: 3, of which 2 were waited for; matrix products, arithmetic and copies ran while one was open for 1% of the time, Pallas kernels for 0%

profile of v1, /device:TPU:1, one launch (start us, length us, event | category | flops | bytes accessed | tf_op | source)
XLA Modules:
  0.0 259.0 jit_solution(5137952515030240151)
XLA Ops:
  7.2 0.0 all-gather.4.cloned.1.call-start
  7.2 0.7 all-gather.4.cloned.1.call-update
  7.9 0.0 all-gather.6.cloned.1.call-start
  7.9 39.3 %all-gather.4.cloned.1.call-done = bf16[8,128,512]{2,1,0:T(8,128)(2,1)} async-done(((bf16[1,128,512]{2,1,0:T(8,128)(2,1)}), bf16[8,128,512]{2,1,0:T(8,128)(2,1)}) %all-gather.4.cloned.1.call-update) | async-done | bytes 1048592 | tf_op jit(solution)/shard_map/all_gather | solution.py:150
  47.2 0.0 all-gather.6.cloned.1.call-update
  47.3 2.6 %broadcast_in_dim.8 = bf16[16,512,128]{2,1,0:T(8,128)(2,1)} broadcast(bf16[512,128]{1,0:T(8,128)(2,1)} %bitcast.12), dimensions={1,2} | broadcast | bytes 2228224 | tf_op jit(solution)/shard_map/broadcast_in_dim | solution.py:15
  49.9 0.0 copy-start.5
  49.9 0.0 copy-start.3
  49.9 0.0 copy-start.4
  49.9 6.7 %all-to-all-start = ((bf16[16,512,128]{2,1,0:T(8,128)(2,1)}), bf16[16,512,128]{2,1,0:T(8,128)(2,1)S(1)}, u32[]{:S(2)}, u32[]{:S(2)}) async-start(bf16[16,512,128]{2,1,0:T(8,128)(2,1)} %broadcast_in_dim.8), calls=%async_computation | async-start | bytes 4194304 | tf_op jit(solution)/shard_map/all_to_all | solution.py:208
  56.6 0.0 copy-done.5
  56.6 0.1 copy.14.tile_list
  56.7 22.7 %all-to-all-done.strip = bf16[16,512,128]{2,1,0:T(8,128)(2,1)S(1)} async-done(((bf16[16,512,128]{2,1,0:T(8,128)(2,1)}), bf16[16,512,128]{2,1,0:T(8,128)(2,1)S(1)}, u32[]{:S(2)}, u32[]{:S(2)}) %all-to-all-start) | async-done | bytes 2097184 | tf_op jit(solution)/shard_map/all_to_all | solution.py:208
  79.4 0.0 all-gather.6.cloned.1.call-done
  79.4 0.0 copy-done.3
  79.4 0.0 copy-done.4
  79.4 0.0 copy-start
  79.4 1.6 copy-done
  81.0 0.0 copy-start.1
  81.0 3.1 %shard_map.68 = f32[16,5,8,256]{3,2,1,0:T(8,128)S(1)} custom-call(s32[128,4]{1,0:T(8,128)S(1)} %copy.14.tile_list, bf16[16,512,128]{2,1,0:T(8,128)(2,1)S(1)} %all-to-all-done.strip, bf16[2,8,128,512]{3,2,1,0:T(8,128)(2,1)S(1)} %bitcast.8, f32[1,128]{1,0:T(1,128)S(1)} %copy-done.3, s32[1,128]{1,0:T(1,128)S(1)} %copy-done.4), custom_call_target="tpu_custom_call" | custom-call | tf_op jit(solution)/shard_map/pallas_call | solution.py:209
  84.1 32.0 %all_to_all.30.arrived = f32[16,5,8,256]{3,2,1,0:T(8,128)S(1)} all-to-all(f32[16,5,8,256]{3,2,1,0:T(8,128)S(1)} %shard_map.68), channel_id=1, replica_groups=mesh['row'=8,'col'=16,'grid'=2] {'row','grid'}, dimensions={0} | all-to-all | bytes 1310720 | tf_op jit(solution)/shard_map/all_to_all | solution.py:210
  116.1 0.0 copy-done.1
  116.1 3.9 %shard_map.69 = bf16[16,512,128]{2,1,0:T(8,128)(2,1)S(1)} custom-call(s32[128,4]{1,0:T(8,128)S(1)} %copy.14.tile_list, f32[16,5,8,256]{3,2,1,0:T(8,128)S(1)} %all_to_all.30.arrived, bf16[2,8,128,512]{3,2,1,0:T(8,128)(2,1)S(1)} %bitcast.9), custom_call_target="tpu_custom_call" | custom-call | tf_op jit(solution)/shard_map/pallas_call | solution.py:211
  120.0 0.0 copy-start.2
  120.0 33.1 %all_to_all.31.pieces = bf16[16,512,128]{2,1,0:T(8,128)(2,1)S(1)} all-to-all(bf16[16,512,128]{2,1,0:T(8,128)(2,1)S(1)} %shard_map.69), channel_id=1, replica_groups=mesh['row'=8,'col'=16,'grid'=2] {'col'}, dimensions={0} | all-to-all | bytes 4194304 | tf_op jit(solution)/shard_map/all_to_all | solution.py:212
  153.1 0.0 copy-done.2
  153.1 1.7 shard_map.70
  154.8 29.7 %all_to_all.32.strip = bf16[16,512,128]{2,1,0:T(8,128)(2,1)S(1)} all-to-all(bf16[16,512,128]{2,1,0:T(8,128)(2,1)S(1)} %get-tuple-element.5), channel_id=1, replica_groups=mesh['row'=8,'col'=16,'grid'=2] {'col'}, dimensions={0} | all-to-all | bytes 4194304 | tf_op jit(solution)/shard_map/all_to_all | solution.py:208
  184.5 3.1 %shard_map.71 = f32[16,5,8,256]{3,2,1,0:T(8,128)S(1)} custom-call(s32[128,4]{1,0:T(8,128)S(1)} %copy.14.tile_list, bf16[16,512,128]{2,1,0:T(8,128)(2,1)S(1)} %all_to_all.32.strip, bf16[2,8,128,512]{3,2,1,0:T(8,128)(2,1)S(1)} %bitcast.10, f32[1,128]{1,0:T(1,128)S(1)} %copy-done.3, s32[1,128]{1,0:T(1,128)S(1)} %copy-done.4), custom_call_target="tpu_custom_call" | custom-call | tf_op jit(solution)/shard_map/pallas_call | solution.py:209
  187.6 26.2 %all_to_all.33.arrived = f32[16,5,8,256]{3,2,1,0:T(8,128)S(1)} all-to-all(f32[16,5,8,256]{3,2,1,0:T(8,128)S(1)} %shard_map.71), channel_id=1, replica_groups=mesh['row'=8,'col'=16,'grid'=2] {'row','grid'}, dimensions={0} | all-to-all | bytes 1310720 | tf_op jit(solution)/shard_map/all_to_all | solution.py:210
  213.9 3.9 %shard_map.72 = bf16[16,512,128]{2,1,0:T(8,128)(2,1)S(1)} custom-call(s32[128,4]{1,0:T(8,128)S(1)} %copy.14.tile_list, f32[16,5,8,256]{3,2,1,0:T(8,128)S(1)} %all_to_all.33.arrived, bf16[2,8,128,512]{3,2,1,0:T(8,128)(2,1)S(1)} %bitcast.11), custom_call_target="tpu_custom_call" | custom-call | tf_op jit(solution)/shard_map/pallas_call | solution.py:211
  217.7 32.8 %all_to_all.34.pieces = bf16[16,512,128]{2,1,0:T(8,128)(2,1)S(1)} all-to-all(bf16[16,512,128]{2,1,0:T(8,128)(2,1)S(1)} %shard_map.72), channel_id=1, replica_groups=mesh['row'=8,'col'=16,'grid'=2] {'col'}, dimensions={0} | all-to-all | bytes 4194304 | tf_op jit(solution)/shard_map/all_to_all | solution.py:212
  250.5 1.6 shard_map.73
Async XLA Ops:
  7.2 40.1 %all-gather.4.cloned.1.call-start = ((), (), s32[]{:S(2)}) async-start(), calls=%async_computation.6 | async-start | bytes 1179648 | tf_op jit(solution)/shard_map/all_gather | solution.py:150
  7.9 71.5 %all-gather.6.cloned.1.call-start = ((), (), s32[]{:S(2)}) async-start(), calls=%async_computation.7 | async-start | bytes 3145728 | tf_op jit(solution)/shard_map/all_gather | solution.py:151
  49.9 6.7 %copy-start.5 = (s32[128,4]{0,1:T(4,128)S(1)}, s32[128,4]{0,1:T(4,128)}, u32[]{:S(2)}) copy-start(s32[128,4]{0,1:T(4,128)} %param.9) | copy-start | bytes 6148
  49.9 29.5 %copy-start.3 = (f32[1,128]{1,0:T(1,128)S(1)}, f32[1,128]{1,0:T(1,128)}, u32[]{:S(2)}) copy-start(f32[1,128]{1,0:T(1,128)} %weight.3) | copy-start | bytes 1540
  49.9 29.5 %copy-start.4 = (s32[1,128]{1,0:T(1,128)S(1)}, s32[1,128]{1,0:T(1,128)}, u32[]{:S(2)}) copy-start(s32[1,128]{1,0:T(1,128)} %screen.3) | copy-start | bytes 1540
  49.9 29.5 %all-to-all-start = ((bf16[16,512,128]{2,1,0:T(8,128)(2,1)}), bf16[16,512,128]{2,1,0:T(8,128)(2,1)S(1)}, u32[]{:S(2)}, u32[]{:S(2)}) async-start(bf16[16,512,128]{2,1,0:T(8,128)(2,1)} %broadcast_in_dim.8), calls=%async_computation | async-start | bytes 4194304 | tf_op jit(solution)/shard_map/all_to_all | solution.py:208
  79.4 1.6 copy-start
  81.0 35.1 %copy-start.1 = (bf16[16,128,512]{2,1,0:T(8,128)(2,1)S(1)}, bf16[16,128,512]{2,1,0:T(8,128)(2,1)}, u32[]{:S(2)}) copy-start(bf16[16,128,512]{2,1,0:T(8,128)(2,1)} %all-gather.6.cloned.1.call-done) | copy-start | bytes 6291460
  120.0 33.1 %copy-start.2 = (bf16[2,1,4,64,128]{4,3,2,1,0:T(8,128)(2,1)S(1)}, bf16[2,1,4,64,128]{4,3,2,1,0:T(8,128)(2,1)}, u32[]{:S(2)}) copy-start(bf16[2,1,4,64,128]{4,3,2,1,0:T(8,128)(2,1)} %param.5) | copy-start | bytes 393220
Sparse Core Ops, SparseCore 0:
  9.8 37.4 all-gather.3
  49.0 20.2 all-gather.5

commit v2 on v1

--- a/solution.py
+++ b/solution.py
@@ -29,8 +29,8 @@
 
 
 def own_rows(basis, slot, half, tile_width, half_tile):
-    points = basis.shape[0] * basis.shape[2]
-    block = basis[:, 0, :, pl.ds(pl.multiple_of(slot * tile_width, tile_width), tile_width)]
+    points = basis.shape[1] * basis.shape[2]
+    block = basis[0, :, :, pl.ds(pl.multiple_of(slot * tile_width, tile_width), tile_width)]
     block = block.reshape(points, tile_width)
     rows = lax.broadcasted_iota(jnp.int32, (half_tile, tile_width), 0) + half * half_tile
     lanes = lax.broadcasted_iota(jnp.int32, (half_tile, tile_width), 1)
@@ -44,13 +44,11 @@
     my_col = lax.axis_index("col")
     half = lax.axis_index("grid")
     span = comps * half_tile
-    points = basis.shape[0] * basis.shape[2]
+    n_half, half_points, functions = basis.shape[1:]
 
     @pl.when(step == 0)
     def _():
         sums[...] = jnp.zeros_like(sums)
-        own = weight[...] * screen[...].astype(jnp.float32)
-        sums[comps, 0:1, 0 : own.shape[1]] = own
 
     columns, slot, multiple, present = find(tile_list, step * n_col + my_col, n_row, my_row)
 
@@ -59,7 +57,7 @@
         for s, tile in enumerate(columns):
             first = pl.multiple_of(multiple * span, span)
             block[:, s * width : (s + 1) * width] = strip[tile, pl.ds(first, span), :]
-        samples = basis[:, 0].reshape(points, basis.shape[3])
+        samples = basis[0].reshape(n_half * half_points, functions)
         part = lax.dot_general(
             block[...], samples, (((1,), (1,)), ((), ())), preferred_element_type=jnp.float32
         )
@@ -70,45 +68,57 @@
 
     @pl.when(step == pl.num_programs(0) - 1)
     def _():
+        own = weight[...] * screen[...].astype(jnp.float32)
         for dest in range(out.shape[0]):
-            out[dest] = sums[...]
-
-
-def potential_kernel(tile_list, arrived, basis, out, scales, acc, *, n_row, n_col, comps, half_tile, width):
+            h = dest % n_half
+            out[dest, 0:comps] = sums[:, :, h * half_points : (h + 1) * half_points]
+            if out.shape[1] > comps:
+                out[dest, comps] = jnp.broadcast_to(own, out.shape[2:])
+
+
+def scales_of(dens, weights):
+    total = dens[0]
+    spin = [dens[comp] for comp in range(1, dens.shape[0])]
+    norm = jnp.sqrt(1.0 + sum(s * s for s in spin))
+    potentials = [total / jnp.sqrt(1.0 + total * total)] + [s / norm for s in spin]
+    return [potential * weights for potential in potentials]
+
+
+def first_scale_kernel(arrived, scales, weights):
+    comps = scales.shape[0]
+    n_row = weights.shape[0]
+    half = lax.axis_index("grid")
+    n_half = arrived.shape[0] // n_row
+    for q in range(n_row):
+        weights[q : q + 1, :] = arrived[q * n_half + half, comps, 0:1, :]
+    for comp, scale in enumerate(scales_of(jnp.sum(arrived[:, 0:comps], axis=0), weights[...])):
+        scales[comp] = scale
+
+
+def scale_kernel(arrived, weights, scales):
+    for comp, scale in enumerate(scales_of(jnp.sum(arrived[...], axis=0), weights[...])):
+        scales[comp] = scale
+
+
+def potential_kernel(tile_list, own, other, basis, out, scales, acc, *, n_row, n_col, comps, half_tile, width):
     step = pl.program_id(0)
     my_row = lax.axis_index("row")
     my_col = lax.axis_index("col")
     half = lax.axis_index("grid")
     span = comps * half_tile
-    points = basis.shape[0] * basis.shape[2]
-    n_half = basis.shape[0]
-    half_points = basis.shape[2]
+    n_half, half_points, functions = basis.shape[1:]
 
     @pl.when(step == 0)
     def _():
         acc[...] = jnp.zeros_like(acc)
-        dens = jnp.sum(arrived[:, 0:comps], axis=0)
-        total = dens[0]
-        spin = [dens[comp] for comp in range(1, comps)]
-        norm = jnp.sqrt(1.0 + sum(s * s for s in spin))
-        potentials = [total / jnp.sqrt(1.0 + total * total)] + [s / norm for s in spin]
-        weights = jnp.concatenate(
-            [
-                jnp.concatenate(
-                    [arrived[q * n_half + h, comps, 0:1, 0:half_points] for h in range(n_half)], axis=1
-                )
-                for q in range(n_row)
-            ],
-            axis=0,
-        )
-        for comp in range(comps):
-            scales[comp] = potentials[comp] * weights
+        scales[:, :, pl.ds(pl.multiple_of(half * half_points, half_points), half_points)] = own[...]
+        scales[:, :, pl.ds(pl.multiple_of((1 - half) * half_points, half_points), half_points)] = other[...]
 
     columns, slot, multiple, present = find(tile_list, step * n_col + my_col, n_row, my_row)
 
     @pl.when(present)
     def _():
-        samples = basis[:, 0].reshape(points, basis.shape[3])
+        samples = basis[0].reshape(n_half * half_points, functions)
         rows = own_rows(basis, slot, half, width, half_tile)
         weighted = jnp.concatenate(
             [(rows * scales[comp, pl.ds(step, 1), :]).astype(jnp.bfloat16) for comp in range(comps)], axis=0
@@ -144,36 +154,42 @@
     points = half_points * n_grid
     rows = row_tiles * comps * half_tile
     span = comps * half_tile
-    planes = comps + 1
     sizes = dict(n_row=n_row, n_col=n_col, comps=comps, half_tile=half_tile, width=width)
     own = density.reshape(rows, width)
-    basis = lax.all_gather(basis_values, "row", axis=0, tiled=True)
-    basis = lax.all_gather(basis, "grid", axis=0, tiled=False)
+    basis = lax.all_gather(basis_values, ("row", "grid"), axis=0, tiled=True)
+    basis = basis.reshape(n_row, n_grid, half_points, functions)
     params = pltpu.CompilerParams(dimension_semantics=("arbitrary",), vmem_limit_bytes=VMEM_BYTES)
-    basis_spec = pl.BlockSpec((n_grid, 1, half_points, functions), lambda b, t: (0, b, 0, 0))
+    basis_spec = pl.BlockSpec((1, n_grid, half_points, functions), lambda b, t: (b, 0, 0, 0))
     whole = lambda *shape: pl.BlockSpec(shape, lambda b, t: (0,) * len(shape))
-    message = (n_row * n_grid, planes, n_row, points)
-    densities = pl.pallas_call(
-        functools.partial(density_kernel, **sizes),
-        grid_spec=pltpu.PrefetchScalarGridSpec(
-            num_scalar_prefetch=1,
-            grid=(n_row,),
-            in_specs=[whole(n_col, rows, width), basis_spec, whole(1, half_points), whole(1, half_points)],
-            out_specs=whole(*message),
-            scratch_shapes=[
-                pltpu.VMEM((span, functions), jnp.bfloat16),
-                pltpu.VMEM((planes, n_row, points), jnp.float32),
-            ],
-        ),
-        out_shape=jax.ShapeDtypeStruct(message, jnp.float32),
-        compiler_params=params,
-    )
+    scale = jax.ShapeDtypeStruct((comps, n_row, half_points), jnp.float32)
+    kept = jax.ShapeDtypeStruct((n_row, half_points), jnp.float32)
+
+    def densities(planes):
+        message = (n_row * n_grid, planes, n_row, half_points)
+        return pl.pallas_call(
+            functools.partial(density_kernel, **sizes),
+            grid_spec=pltpu.PrefetchScalarGridSpec(
+                num_scalar_prefetch=1,
+                grid=(n_row,),
+                in_specs=[whole(n_col, rows, width), basis_spec, whole(1, half_points), whole(1, half_points)],
+                out_specs=whole(*message),
+                scratch_shapes=[
+                    pltpu.VMEM((span, functions), jnp.bfloat16),
+                    pltpu.VMEM((comps, n_row, points), jnp.float32),
+                ],
+            ),
+            out_shape=jax.ShapeDtypeStruct(message, jnp.float32),
+            compiler_params=params,
+        )
+
+    first_scales = pl.pallas_call(first_scale_kernel, out_shape=[scale, kept])
+    scales = pl.pallas_call(scale_kernel, out_shape=scale)
     potentials = pl.pallas_call(
         functools.partial(potential_kernel, **sizes),
         grid_spec=pltpu.PrefetchScalarGridSpec(
             num_scalar_prefetch=1,
             grid=(n_row,),
-            in_specs=[whole(*message), basis_spec],
+            in_specs=[whole(*scale.shape), whole(*scale.shape), basis_spec],
             out_specs=whole(n_col, rows, width),
             scratch_shapes=[
                 pltpu.VMEM((comps, n_row, points), jnp.float32),
@@ -204,15 +220,18 @@
         compiler_params=params,
     )
 
-    def build(copies):
+    def partials(copies, planes):
         strip = lax.all_to_all(copies, "col", 0, 0, tiled=True)
-        partials = densities(tile_list, strip, basis, quad_weight, screen)
-        arrived = lax.all_to_all(partials, ("row", "grid"), 0, 0, tiled=True)
-        slabs = potentials(tile_list, arrived, basis)
-        return lax.all_to_all(slabs, "col", 0, 0, tiled=True)
-
-    first, copies = update(build(everyone(own, n_col)), own)
-    second = add_up(build(copies))
+        partial = densities(planes)(tile_list, strip, basis, quad_weight, screen)
+        return lax.all_to_all(partial, ("row", "grid"), 0, 0, tiled=True)
+
+    def slabs(mine):
+        other = lax.ppermute(mine, "grid", [(0, 1), (1, 0)])
+        return lax.all_to_all(potentials(tile_list, mine, other, basis), "col", 0, 0, tiled=True)
+
+    mine, weights = first_scales(partials(everyone(own, n_col), comps + 1))
+    first, copies = update(slabs(mine), own)
+    second = add_up(slabs(scales(partials(copies, comps), weights)))
     shape = density.shape
     return first.reshape(shape), second.reshape(shape)
 

time: 260 us -> 219 us (0.84)
  waiting for transfers between devices: 62.7 us -> 37.4 us
  blocking collectives: 154 us -> 129 us
  Pallas kernels: 17.3 us -> 22.4 us
  local copies, waits for them, and re-layouts: 4.36 us -> 8.7 us
    all_gather x2 -> x1, waiting for transfers between devices: 39.3 us -> 6.18 us  [body(): basis = lax.all_gather(basis_values, ('row', 'grid'), axis=0, tiled=True)]
    all_to_all x5, blocking collectives: 154 us -> 129 us  [the longest x2 61.9 us: slabs(): lax.all_to_all(potentials(tile_list, mine, other, basis), 'col', 0, 0, ti...]
    pallas_call x6 -> x8, Pallas kernels: 17.3 us -> 22.4 us  [the longest x2 8.88 us: slabs(): potentials(tile_list, mine, other, basis)]
    all_to_all x1, waiting for transfers between devices: 22.7 us -> 27.8 us  [partials(): strip = lax.all_to_all(copies, 'col', 0, 0, tiled=True)]
    unnamed x13 -> x21, local copies, waits for them, and re-layouts: 1.72 us -> 6.07 us
    ppermute x0 -> x2, waiting for transfers between devices: none -> 2.78 us  [slabs(): other = lax.ppermute(mine, 'grid', [(0, 1), (1, 0)])]
  transfers between devices with their start and end apart: 3 -> 4, of which waited for: 2 -> 4; matrix products, arithmetic and copies ran while one was open for 1% -> 1% of each run, Pallas kernels for 0% -> 0%
where the time goes in v2:
time: 219 us
  blocking collectives  129 us (59%)
  waiting for transfers between devices  37.4 us (17%)
  Pallas kernels  22.4 us (10%)
  between operations  14.1 us (6%)
  local copies, waits for them, and re-layouts  8.7 us (4%)
  starting transfers between devices  7.76 us (4%)
    all_to_all x2, blocking collectives, slabs(): lax.all_to_all(potentials(tile_list, mine, other, basis), 'col', 0, 0, ti...  61.9 us
    all_to_all x2, blocking collectives, partials(): return lax.all_to_all(partial, ('row', 'grid'), 0, 0, tiled=True)  36.9 us
    all_to_all x1, blocking collectives, partials(): strip = lax.all_to_all(copies, 'col', 0, 0, tiled=True)  29.7 us
    all_to_all x1, waiting for transfers between devices, partials(): strip = lax.all_to_all(copies, 'col', 0, 0, tiled=True)  27.8 us
    pallas_call x2, Pallas kernels, slabs(): potentials(tile_list, mine, other, basis)  8.88 us
    all_to_all x1, starting transfers between devices, partials(): strip = lax.all_to_all(copies, 'col', 0, 0, tiled=True)  7.72 us
    pallas_call x2, Pallas kernels, partials(): partial = densities(planes)(tile_list, strip, basis, quad_weight, screen)  7 us
    all_gather x1, waiting for transfers between devices, body(): basis = lax.all_gather(basis_values, ('row', 'grid'), axis=0, tiled=True)  6.18 us
  transfers between devices with their start and end apart: 4, of which 4 were waited for; matrix products, arithmetic and copies ran while one was open for 1% of the time, Pallas kernels for 0%

profile of v2, /device:TPU:1, one launch (start us, length us, event | category | flops | bytes accessed | tf_op | source)
XLA Modules:
  0.0 218.9 jit_solution(4288062055059912346)
XLA Ops:
  7.2 0.0 all-gather.2.cloned.1.call-start
  7.2 0.7 all-gather.2.cloned.1.call-update
  7.9 2.6 %broadcast_in_dim.8 = bf16[16,512,128]{2,1,0:T(8,128)(2,1)} broadcast(bf16[512,128]{1,0:T(8,128)(2,1)} %bitcast.12), dimensions={1,2} | broadcast | bytes 2228224 | tf_op jit(solution)/shard_map/broadcast_in_dim | solution.py:15
  10.5 0.0 copy-start.9
  10.5 0.0 copy-start.7
  10.5 0.0 copy-start.8
  10.5 7.7 %all-to-all-start = ((bf16[16,512,128]{2,1,0:T(8,128)(2,1)}), bf16[16,512,128]{2,1,0:T(8,128)(2,1)S(1)}, u32[]{:S(2)}, u32[]{:S(2)}) async-start(bf16[16,512,128]{2,1,0:T(8,128)(2,1)} %broadcast_in_dim.8), calls=%async_computation | async-start | bytes 4194304 | tf_op jit(solution)/shard_map/all_to_all | solution.py:224
  18.3 0.0 copy-done.9
  18.3 0.1 copy.14.tile_list
  18.4 27.8 %all-to-all-done.strip = bf16[16,512,128]{2,1,0:T(8,128)(2,1)S(1)} async-done(((bf16[16,512,128]{2,1,0:T(8,128)(2,1)}), bf16[16,512,128]{2,1,0:T(8,128)(2,1)S(1)}, u32[]{:S(2)}, u32[]{:S(2)}) %all-to-all-start) | async-done | bytes 2097184 | tf_op jit(solution)/shard_map/all_to_all | solution.py:224
  46.1 0.0 copy-start.2
  46.1 1.3 copy-done.2
  47.5 6.2 %all-gather.2.cloned.1.call-done = bf16[16,128,512]{2,1,0:T(8,128)(2,1)} async-done(((bf16[1,128,512]{2,1,0:T(8,128)(2,1)}), bf16[16,128,512]{2,1,0:T(8,128)(2,1)}) %all-gather.2.cloned.1.call-update) | async-done | bytes 2097168 | tf_op jit(solution)/shard_map/all_gather | solution.py:159
  53.6 0.0 copy-done.7
  53.6 0.0 copy-done.8
  53.6 0.0 copy-start
  53.6 1.6 copy-done
  55.2 0.0 copy-start.3
  55.2 1.6 copy-done.3
  56.8 0.0 copy-start.1
  56.8 3.5 %shard_map.68 = f32[16,5,8,128]{3,2,1,0:T(8,128)S(1)} custom-call(s32[128,4]{1,0:T(8,128)S(1)} %copy.14.tile_list, bf16[16,512,128]{2,1,0:T(8,128)(2,1)S(1)} %copy-done.3, bf16[8,2,128,512]{3,2,1,0:T(8,128)(2,1)S(1)} %bitcast.8, f32[1,128]{1,0:T(1,128)S(1)} %copy-done.7, s32[1,128]{1,0:T(1,128)S(1)} %copy-done.8), custom_call_target="tpu_custom_call" | custom-call | tf_op jit(solution)/shard_map/pallas_call | solution.py:225
  60.3 18.4 %all_to_all.30.arrived = f32[16,5,8,128]{3,2,1,0:T(8,128)} all-to-all(f32[16,5,8,128]{3,2,1,0:T(8,128)S(1)} %shard_map.68), channel_id=1, replica_groups=mesh['row'=8,'col'=16,'grid'=2] {'row','grid'}, dimensions={0} | all-to-all | bytes 655360 | tf_op jit(solution)/shard_map/all_to_all | solution.py:226
  78.8 1.6 shard_map.69
  80.4 0.0 collective-permute-start
  80.4 1.4 collective-permute-done.other
  81.8 0.0 copy-done.1
  81.8 0.0 copy-start.6
  81.8 0.7 copy-done.6
  82.5 4.4 %shard_map.70 = bf16[16,512,128]{2,1,0:T(8,128)(2,1)S(1)} custom-call(s32[128,4]{1,0:T(8,128)S(1)} %copy.14.tile_list, f32[4,8,128]{2,1,0:T(8,128)S(1)} %copy-done.6, f32[4,8,128]{2,1,0:T(8,128)S(1)} %collective-permute-done.other, bf16[8,2,128,512]{3,2,1,0:T(8,128)(2,1)S(1)} %bitcast.9), custom_call_target="tpu_custom_call" | custom-call | tf_op jit(solution)/shard_map/pallas_call | solution.py:230
  87.0 0.0 copy-start.4
  87.0 32.2 %all_to_all.31.pieces = bf16[16,512,128]{2,1,0:T(8,128)(2,1)S(1)} all-to-all(bf16[16,512,128]{2,1,0:T(8,128)(2,1)S(1)} %shard_map.70), channel_id=1, replica_groups=mesh['row'=8,'col'=16,'grid'=2] {'col'}, dimensions={0} | all-to-all | bytes 4194304 | tf_op jit(solution)/shard_map/all_to_all | solution.py:230
  119.2 0.0 copy-done.4
  119.2 1.7 shard_map.71
  120.9 29.7 %all_to_all.32.strip = bf16[16,512,128]{2,1,0:T(8,128)(2,1)S(1)} all-to-all(bf16[16,512,128]{2,1,0:T(8,128)(2,1)S(1)} %get-tuple-element.8), channel_id=1, replica_groups=mesh['row'=8,'col'=16,'grid'=2] {'col'}, dimensions={0} | all-to-all | bytes 4194304 | tf_op jit(solution)/shard_map/all_to_all | solution.py:224
  150.5 3.5 %shard_map.72 = f32[16,4,8,128]{3,2,1,0:T(8,128)S(1)} custom-call(s32[128,4]{1,0:T(8,128)S(1)} %copy.14.tile_list, bf16[16,512,128]{2,1,0:T(8,128)(2,1)S(1)} %all_to_all.32.strip, bf16[8,2,128,512]{3,2,1,0:T(8,128)(2,1)S(1)} %bitcast.10, f32[1,128]{1,0:T(1,128)S(1)} %copy-done.7, s32[1,128]{1,0:T(1,128)S(1)} %copy-done.8), custom_call_target="tpu_custom_call" | custom-call | tf_op jit(solution)/shard_map/pallas_call | solution.py:225
  154.1 18.5 %all_to_all.33.arrived = f32[16,4,8,128]{3,2,1,0:T(8,128)} all-to-all(f32[16,4,8,128]{3,2,1,0:T(8,128)S(1)} %shard_map.72), channel_id=1, replica_groups=mesh['row'=8,'col'=16,'grid'=2] {'row','grid'}, dimensions={0} | all-to-all | bytes 524288 | tf_op jit(solution)/shard_map/all_to_all | solution.py:226
  172.6 1.6 shard_map.73.own
  174.2 0.0 collective-permute-start.1
  174.2 1.4 collective-permute-done.1.other
  175.6 0.0 copy-start.5
  175.6 0.7 copy-done.5
  176.3 4.4 %shard_map.74 = bf16[16,512,128]{2,1,0:T(8,128)(2,1)S(1)} custom-call(s32[128,4]{1,0:T(8,128)S(1)} %copy.14.tile_list, f32[4,8,128]{2,1,0:T(8,128)S(1)} %copy-done.5, f32[4,8,128]{2,1,0:T(8,128)S(1)} %collective-permute-done.1.other, bf16[8,2,128,512]{3,2,1,0:T(8,128)(2,1)S(1)} %bitcast.11), custom_call_target="tpu_custom_call" | custom-call | tf_op jit(solution)/shard_map/pallas_call | solution.py:230
  180.7 29.7 %all_to_all.34.pieces = bf16[16,512,128]{2,1,0:T(8,128)(2,1)S(1)} all-to-all(bf16[16,512,128]{2,1,0:T(8,128)(2,1)S(1)} %shard_map.74), channel_id=1, replica_groups=mesh['row'=8,'col'=16,'grid'=2] {'col'}, dimensions={0} | all-to-all | bytes 4194304 | tf_op jit(solution)/shard_map/all_to_all | solution.py:230
  210.4 1.6 shard_map.75
Async XLA Ops:
  7.2 46.5 %all-gather.2.cloned.1.call-start = ((), (), s32[]{:S(2)}) async-start(), calls=%async_computation.6 | async-start | bytes 2228224 | tf_op jit(solution)/shard_map/all_gather | solution.py:159
  10.5 7.7 %copy-start.9 = (s32[128,4]{0,1:T(4,128)S(1)}, s32[128,4]{0,1:T(4,128)}, u32[]{:S(2)}) copy-start(s32[128,4]{0,1:T(4,128)} %param.9) | copy-start | bytes 6148
  10.5 43.1 %copy-start.7 = (f32[1,128]{1,0:T(1,128)S(1)}, f32[1,128]{1,0:T(1,128)}, u32[]{:S(2)}) copy-start(f32[1,128]{1,0:T(1,128)} %weight.3) | copy-start | bytes 1540
  10.5 43.1 %copy-start.8 = (s32[1,128]{1,0:T(1,128)S(1)}, s32[1,128]{1,0:T(1,128)}, u32[]{:S(2)}) copy-start(s32[1,128]{1,0:T(1,128)} %screen.3) | copy-start | bytes 1540
  10.5 35.6 %all-to-all-start = ((bf16[16,512,128]{2,1,0:T(8,128)(2,1)}), bf16[16,512,128]{2,1,0:T(8,128)(2,1)S(1)}, u32[]{:S(2)}, u32[]{:S(2)}) async-start(bf16[16,512,128]{2,1,0:T(8,128)(2,1)} %broadcast_in_dim.8), calls=%async_computation | async-start | bytes 4194304 | tf_op jit(solution)/shard_map/all_to_all | solution.py:224
  46.1 1.3 copy-start.2
  53.6 1.6 copy-start
  55.2 1.6 copy-start.3
  56.8 25.0 %copy-start.1 = (bf16[16,128,512]{2,1,0:T(8,128)(2,1)S(1)}, bf16[16,128,512]{2,1,0:T(8,128)(2,1)}, u32[]{:S(2)}) copy-start(bf16[16,128,512]{2,1,0:T(8,128)(2,1)} %all-gather.2.cloned.1.call-done) | copy-start | bytes 6291460
  80.4 1.4 collective-permute-start
  81.8 0.7 copy-start.6
  87.0 32.2 %copy-start.4 = (bf16[2,1,4,64,128]{4,3,2,1,0:T(8,128)(2,1)S(1)}, bf16[2,1,4,64,128]{4,3,2,1,0:T(8,128)(2,1)}, u32[]{:S(2)}) copy-start(bf16[2,1,4,64,128]{4,3,2,1,0:T(8,128)(2,1)} %param.5) | copy-start | bytes 393220
  174.2 1.4 collective-permute-start.1
  175.6 0.7 copy-start.5
Sparse Core Ops, SparseCore 0:
  9.8 43.7 all-gather.1

commit v3 on v2

v3 whole, which is shorter than its diff:
```python
import functools

import jax
import jax.numpy as jnp
from jax import lax
from jax.experimental import pallas as pl
from jax.experimental.pallas import tpu as pltpu
from jax.sharding import PartitionSpec as P

MIXING = 0.001
VMEM_BYTES = 32 * 1024 * 1024


def everyone(x, n):
    return jnp.broadcast_to(x[None], (n, *x.shape))


def find(tile_list, batch, n_row, my_row):
    columns = [tile_list[batch, s] for s in range(tile_list.shape[1])]
    slot = jnp.int32(0)
    multiple = jnp.int32(0)
    present = jnp.bool_(False)
    for s, tile in enumerate(columns):
        match = lax.rem(tile, n_row) == my_row
        slot = jnp.where(match, s, slot)
        multiple = jnp.where(match, lax.div(tile, n_row), multiple)
        present = jnp.logical_or(present, match)
    return columns, slot, multiple, present


def own_rows(basis, batch, slot, half, tile_width, half_tile):
    points = basis.shape[1] * basis.shape[2]
    block = basis[batch, :, :, pl.ds(pl.multiple_of(slot * tile_width, tile_width), tile_width)]
    block = block.reshape(points, tile_width)
    rows = lax.broadcasted_iota(jnp.int32, (half_tile, tile_width), 0) + half * half_tile
    lanes = lax.broadcasted_iota(jnp.int32, (half_tile, tile_width), 1)
    chosen = jnp.where(rows == lanes, 1.0, 0.0).astype(jnp.bfloat16)
    return lax.dot_general(chosen, block, (((1,), (1,)), ((), ())), preferred_element_type=jnp.float32)


def add_densities(tile_list, strip, basis, arrival, weight, screen, out, sums, *, n_col, comps, half_tile, width):
    my_row = lax.axis_index("row")
    my_col = lax.axis_index("col")
    half = lax.axis_index("grid")
    span = comps * half_tile
    n_row, n_half, half_points, functions = basis.shape
    for batch in range(n_row):
        arrival(batch)
        columns, slot, multiple, present = find(tile_list, batch * n_col + my_col, n_row, my_row)
        first = pl.multiple_of(multiple * span, span)
        block = jnp.concatenate([strip[tile, pl.ds(first, span), :] for tile in columns], axis=1)
        samples = basis[batch].reshape(n_half * half_points, functions)
        part = lax.dot_general(block, samples, (((1,), (1,)), ((), ())), preferred_element_type=jnp.float32)
        rows = own_rows(basis, batch, slot, half, width, half_tile)
        for comp in range(comps):
            piece = part[comp * half_tile : (comp + 1) * half_tile, :] * rows
            total = jnp.sum(piece, axis=0, keepdims=True)
            sums[comp, batch : batch + 1, :] = jnp.where(present, total, 0.0)
    own = weight[...] * screen[...].astype(jnp.float32)
    for dest in range(out.shape[0]):
        h = dest % n_half
        out[dest, 0:comps] = sums[:, :, h * half_points : (h + 1) * half_points]
        if out.shape[1] > comps:
            out[dest, comps] = jnp.broadcast_to(own, out.shape[2:])


def first_density_kernel(tile_list, strip_far, basis_far, weight, screen, out, strip, basis, sums, sems, **sizes):
    n_row = basis.shape[0]
    strip_copy = pltpu.make_async_copy(strip_far, strip, sems.at[n_row])
    basis_copies = [
        pltpu.make_async_copy(basis_far.at[batch], basis.at[batch], sems.at[batch]) for batch in range(n_row)
    ]
    strip_copy.start()
    for copy in basis_copies:
        copy.start()
    strip_copy.wait()
    arrival = lambda batch: basis_copies[batch].wait()
    add_densities(tile_list, strip, basis, arrival, weight, screen, out, sums, **sizes)


def density_kernel(tile_list, strip, basis, weight, screen, out, sums, **sizes):
    add_densities(tile_list, strip, basis, lambda batch: None, weight, screen, out, sums, **sizes)


def scales_of(dens, weights):
    total = dens[0]
    spin = [dens[comp] for comp in range(1, dens.shape[0])]
    norm = jnp.sqrt(1.0 + sum(s * s for s in spin))
    potentials = [total / jnp.sqrt(1.0 + total * total)] + [s / norm for s in spin]
    return [potential * weights for potential in potentials]


def first_scale_kernel(arrived, scales, weights):
    comps = scales.shape[0]
    n_row = weights.shape[0]
    half = lax.axis_index("grid")
    n_half = arrived.shape[0] // n_row
    for q in range(n_row):
        weights[q : q + 1, :] = arrived[q * n_half + half, comps, 0:1, :]
    for comp, scale in enumerate(scales_of(jnp.sum(arrived[:, 0:comps], axis=0), weights[...])):
        scales[comp] = scale


def scale_kernel(arrived, weights, scales):
    for comp, scale in enumerate(scales_of(jnp.sum(arrived[...], axis=0), weights[...])):
        scales[comp] = scale


def potential_kernel(tile_list, own, other, basis, out, scales, acc, seen, *, n_col, comps, half_tile, width):
    my_row = lax.axis_index("row")
    my_col = lax.axis_index("col")
    half = lax.axis_index("grid")
    span = comps * half_tile
    n_row, n_half, half_points, functions = basis.shape
    for tile in range(acc.shape[0]):
        for multiple in range(acc.shape[1] // span):
            seen[tile, multiple] = 0
    scales[:, :, pl.ds(pl.multiple_of(half * half_points, half_points), half_points)] = own[...]
    scales[:, :, pl.ds(pl.multiple_of((1 - half) * half_points, half_points), half_points)] = other[...]

    for batch in range(n_row):
        columns, slot, multiple, present = find(tile_list, batch * n_col + my_col, n_row, my_row)
        samples = basis[batch].reshape(n_half * half_points, functions)
        rows = own_rows(basis, batch, slot, half, width, half_tile)
        rows = jnp.where(present, rows, 0.0)
        weighted = jnp.concatenate(
            [(rows * scales[comp, batch : batch + 1, :]).astype(jnp.bfloat16) for comp in range(comps)], axis=0
        )
        part = jnp.dot(weighted, samples, preferred_element_type=jnp.float32)
        first = pl.multiple_of(multiple * span, span)
        for s, tile in enumerate(columns):
            before = jnp.where(seen[tile, multiple] > 0, acc[tile, pl.ds(first, span), :], 0.0)
            acc[tile, pl.ds(first, span), :] = before + part[:, s * width : (s + 1) * width]
            seen[tile, multiple] = 1
    for tile in range(acc.shape[0]):
        for multiple in range(acc.shape[1] // span):
            rows = slice(multiple * span, (multiple + 1) * span)
            out[tile, rows, :] = jnp.where(seen[tile, multiple] > 0, acc[tile, rows, :], 0.0).astype(jnp.bfloat16)


def update_kernel(pieces, density, first, copies):
    total = jnp.sum(pieces[...].astype(jnp.float32), axis=0).astype(jnp.bfloat16)
    first[...] = total
    updated = (density[...].astype(jnp.float32) + MIXING * total.astype(jnp.float32)).astype(jnp.bfloat16)
    for dest in range(copies.shape[0]):
        copies[dest] = updated


def sum_kernel(pieces, out):
    out[...] = jnp.sum(pieces[...].astype(jnp.float32), axis=0).astype(jnp.bfloat16)


def body(density, basis_values, quad_weight, screen, tile_list):
    n_row = lax.axis_size("row")
    n_col = lax.axis_size("col")
    n_grid = lax.axis_size("grid")
    row_tiles, _, comps, half_tile, width = density.shape
    half_points, functions = basis_values.shape[1:]
    points = half_points * n_grid
    rows = row_tiles * comps * half_tile
    span = comps * half_tile
    sizes = dict(n_col=n_col, comps=comps, half_tile=half_tile, width=width)
    own = density.reshape(rows, width)
    basis = lax.all_gather(basis_values, ("row", "grid"), axis=0, tiled=True)
    basis = basis.reshape(n_row, n_grid, half_points, functions)
    params = pltpu.CompilerParams(vmem_limit_bytes=VMEM_BYTES)
    in_smem = pl.BlockSpec(memory_space=pltpu.SMEM)
    in_vmem = pl.BlockSpec(memory_space=pltpu.VMEM)
    scale = jax.ShapeDtypeStruct((comps, n_row, half_points), jnp.float32)
    kept = jax.ShapeDtypeStruct((n_row, half_points), jnp.float32)

    in_hbm = pl.BlockSpec(memory_space=pltpu.HBM)
    sums = pltpu.VMEM((comps, n_row, points), jnp.float32)
    message = lambda planes: jax.ShapeDtypeStruct((n_row * n_grid, planes, n_row, half_points), jnp.float32)
    first_densities = pl.pallas_call(
        functools.partial(first_density_kernel, **sizes),
        in_specs=[in_smem, in_hbm, in_hbm, in_vmem, in_vmem],
        out_specs=in_vmem,
        scratch_shapes=[
            pltpu.VMEM((n_col, rows, width), jnp.bfloat16),
            pltpu.VMEM((n_row, n_grid, half_points, functions), jnp.bfloat16),
            sums,
            pltpu.SemaphoreType.DMA((n_row + 1,)),
        ],
        out_shape=message(comps + 1),
        compiler_params=params,
    )
    densities = pl.pallas_call(
        functools.partial(density_kernel, **sizes),
        in_specs=[in_smem, in_vmem, in_vmem, in_vmem, in_vmem],
        out_specs=in_vmem,
        scratch_shapes=[sums],
        out_shape=message(comps),
        compiler_params=params,
    )
    first_scales = pl.pallas_call(
        first_scale_kernel, in_specs=[in_vmem], out_specs=[in_vmem, in_vmem], out_shape=[scale, kept]
    )
    scales = pl.pallas_call(scale_kernel, in_specs=[in_vmem, in_vmem], out_specs=in_vmem, out_shape=scale)
    potentials = pl.pallas_call(
        functools.partial(potential_kernel, **sizes),
        in_specs=[in_smem, in_vmem, in_vmem, in_vmem],
        out_specs=in_vmem,
        scratch_shapes=[
            pltpu.VMEM((comps, n_row, points), jnp.float32),
            pltpu.VMEM((n_col, rows, width), jnp.float32),
            pltpu.SMEM((n_col, row_tiles), jnp.int32),
        ],
        out_shape=jax.ShapeDtypeStruct((n_col, rows, width), jnp.bfloat16),
        compiler_params=params,
    )
    owned = jax.ShapeDtypeStruct((rows, width), jnp.bfloat16)
    update = pl.pallas_call(
        update_kernel,
        in_specs=[in_vmem, in_vmem],
        out_specs=[in_vmem, in_vmem],
        out_shape=[owned, jax.ShapeDtypeStruct((n_col, rows, width), jnp.bfloat16)],
        compiler_params=params,
    )
    add_up = pl.pallas_call(
        sum_kernel, in_specs=[in_vmem], out_specs=in_vmem, out_shape=owned, compiler_params=params
    )

    def partials(kernel, copies, space):
        strip = lax.all_to_all(copies, "col", 0, 0, tiled=True)
        operands = [pltpu.with_memory_space_constraint(x, space) for x in (strip, basis)]
        partial = kernel(tile_list, *operands, quad_weight, screen)
        arrived = lax.all_to_all(partial, ("row", "grid"), 0, 0, tiled=True)
        return pltpu.with_memory_space_constraint(arrived, pltpu.VMEM)

    def slabs(mine):
        other = lax.ppermute(mine, "grid", [(0, 1), (1, 0)])
        return lax.all_to_all(potentials(tile_list, mine, other, basis), "col", 0, 0, tiled=True)

    mine, weights = first_scales(partials(first_densities, everyone(own, n_col), pltpu.HBM))
    first, copies = update(slabs(mine), own)
    second = add_up(slabs(scales(partials(densities, copies, pltpu.VMEM), weights)))
    shape = density.shape
    return first.reshape(shape), second.reshape(shape)


def solution(mesh):
    in_specs = (
        P(None, "row", None, "grid", "col"),
        P(("row", "col"), "grid", None),
        P(("row", "col"), "grid"),
        P(("row", "col"), "grid"),
        P(),
    )
    out_specs = (P(None, "row", None, "grid", "col"), P(None, "row", None, "grid", "col"))
    return jax.shard_map(body, mesh=mesh, in_specs=in_specs, out_specs=out_specs, check_vma=False)
```

time: 219 us -> 214 us (0.977)
  local copies, waits for them, and re-layouts: 8.7 us -> 4.21 us
    unnamed x21 -> x17, local copies, waits for them, and re-layouts: 6.07 us -> 1.57 us
where the time goes in v3:
time: 214 us
  blocking collectives  129 us (60%)
  waiting for transfers between devices  38.7 us (18%)
  Pallas kernels  20.4 us (10%)
  between operations  14.1 us (7%)
  starting transfers between devices  7.76 us (4%)
  local copies, waits for them, and re-layouts  4.21 us (2%)
    all_to_all x2, blocking collectives, slabs(): lax.all_to_all(potentials(tile_list, mine, other, basis), 'col', 0, 0, ti...  62.4 us
    all_to_all x2, blocking collectives, partials(): arrived = lax.all_to_all(partial, ('row', 'grid'), 0, 0, tiled=True)  36.4 us
    all_to_all x1, blocking collectives, partials(): strip = lax.all_to_all(copies, 'col', 0, 0, tiled=True)  29.7 us
    all_to_all x1, waiting for transfers between devices, partials(): strip = lax.all_to_all(copies, 'col', 0, 0, tiled=True)  27.8 us
    pallas_call x2, Pallas kernels, partials(): partial = kernel(tile_list, *operands, quad_weight, screen)  8.63 us
    pallas_call x2, Pallas kernels, slabs(): potentials(tile_list, mine, other, basis)  7.84 us
    all_to_all x1, starting transfers between devices, partials(): strip = lax.all_to_all(copies, 'col', 0, 0, tiled=True)  7.72 us
    all_gather x1, waiting for transfers between devices, body(): basis = lax.all_gather(basis_values, ('row', 'grid'), axis=0, tiled=True)  7.49 us
  transfers between devices with their start and end apart: 4, of which 4 were waited for; matrix products, arithmetic and copies ran while one was open for 1% of the time, Pallas kernels for 0%

profile of v3, /device:TPU:1, one launch (start us, length us, event | category | flops | bytes accessed | tf_op | source)
XLA Modules:
  0.0 213.7 jit_solution(15873752731453535430)
XLA Ops:
  7.2 0.0 all-gather.2.cloned.1.call-start
  7.2 0.7 all-gather.2.cloned.1.call-update
  7.9 2.6 %broadcast_in_dim.8 = bf16[16,512,128]{2,1,0:T(8,128)(2,1)} broadcast(bf16[512,128]{1,0:T(8,128)(2,1)} %bitcast.12), dimensions={1,2} | broadcast | bytes 2228224 | tf_op jit(solution)/shard_map/broadcast_in_dim | solution.py:15
  10.5 0.0 copy-start.7
  10.5 0.0 copy-start.4
  10.5 0.0 copy-start.5
  10.5 7.7 %all-to-all-start = ((bf16[16,512,128]{2,1,0:T(8,128)(2,1)}), bf16[16,512,128]{2,1,0:T(8,128)(2,1)S(1)}, u32[]{:S(2)}, u32[]{:S(2)}) async-start(bf16[16,512,128]{2,1,0:T(8,128)(2,1)} %broadcast_in_dim.8), calls=%async_computation | async-start | bytes 4194304 | tf_op jit(solution)/shard_map/all_to_all | solution.py:225
  18.3 0.0 copy-done.7
  18.3 0.1 copy.14.tile_list
  18.4 27.8 %all-to-all-done.strip_far = bf16[16,512,128]{2,1,0:T(8,128)(2,1)S(1)} async-done(((bf16[16,512,128]{2,1,0:T(8,128)(2,1)}), bf16[16,512,128]{2,1,0:T(8,128)(2,1)S(1)}, u32[]{:S(2)}, u32[]{:S(2)}) %all-to-all-start) | async-done | bytes 2097184 | tf_op jit(solution)/shard_map/all_to_all | solution.py:225
  46.1 0.0 copy-start.6
  46.2 7.5 %all-gather.2.cloned.1.call-done = bf16[16,128,512]{2,1,0:T(8,128)(2,1)} async-done(((bf16[1,128,512]{2,1,0:T(8,128)(2,1)}), bf16[16,128,512]{2,1,0:T(8,128)(2,1)}) %all-gather.2.cloned.1.call-update) | async-done | bytes 2097168 | tf_op jit(solution)/shard_map/all_gather | solution.py:164
  53.6 0.0 copy-done.6
  53.6 0.0 copy-done.4
  53.6 0.0 copy-done.5
  53.6 0.0 copy-start
  53.7 6.0 %shard_map.68 = f32[16,5,8,128]{3,2,1,0:T(8,128)S(1)} custom-call(s32[128,4]{1,0:T(8,128)S(1)} %copy.14.tile_list, bf16[16,512,128]{2,1,0:T(8,128)(2,1)} %copy-done.6, bf16[8,2,128,512]{3,2,1,0:T(8,128)(2,1)} %bitcast.8, f32[1,128]{1,0:T(1,128)S(1)} %copy-done.4, s32[1,128]{1,0:T(1,128)S(1)} %copy-done.5), custom_call_target="tpu_custom_call" | custom-call | tf_op jit(solution)/shard_map/pallas_call | solution.py:227
  59.7 18.6 %all_to_all.30.arrived = f32[16,5,8,128]{3,2,1,0:T(8,128)S(1)} all-to-all(f32[16,5,8,128]{3,2,1,0:T(8,128)S(1)} %shard_map.68), channel_id=1, replica_groups=mesh['row'=8,'col'=16,'grid'=2] {'row','grid'}, dimensions={0} | all-to-all | bytes 655360 | tf_op jit(solution)/shard_map/all_to_all | solution.py:228
  78.3 0.6 shard_map.69
  78.9 0.0 collective-permute-start
  79.0 1.4 collective-permute-done.other
  80.3 0.0 copy-done
  80.3 0.0 copy-start.3
  80.3 0.7 copy-done.3
  81.1 3.9 %shard_map.70 = bf16[16,512,128]{2,1,0:T(8,128)(2,1)S(1)} custom-call(s32[128,4]{1,0:T(8,128)S(1)} %copy.14.tile_list, f32[4,8,128]{2,1,0:T(8,128)S(1)} %copy-done.3, f32[4,8,128]{2,1,0:T(8,128)S(1)} %collective-permute-done.other, bf16[8,2,128,512]{3,2,1,0:T(8,128)(2,1)S(1)} %bitcast.9), custom_call_target="tpu_custom_call" | custom-call | tf_op jit(solution)/shard_map/pallas_call | solution.py:233
  85.0 0.0 copy-start.1
  85.0 32.4 %all_to_all.31.pieces = bf16[16,512,128]{2,1,0:T(8,128)(2,1)S(1)} all-to-all(bf16[16,512,128]{2,1,0:T(8,128)(2,1)S(1)} %shard_map.70), channel_id=1, replica_groups=mesh['row'=8,'col'=16,'grid'=2] {'col'}, dimensions={0} | all-to-all | bytes 4194304 | tf_op jit(solution)/shard_map/all_to_all | solution.py:233
  117.4 0.0 copy-done.1
  117.4 1.0 shard_map.71
  118.4 29.7 %all_to_all.32.strip = bf16[16,512,128]{2,1,0:T(8,128)(2,1)S(1)} all-to-all(bf16[16,512,128]{2,1,0:T(8,128)(2,1)S(1)} %get-tuple-element.8), channel_id=1, replica_groups=mesh['row'=8,'col'=16,'grid'=2] {'col'}, dimensions={0} | all-to-all | bytes 4194304 | tf_op jit(solution)/shard_map/all_to_all | solution.py:225
  148.1 2.6 %shard_map.72 = f32[16,4,8,128]{3,2,1,0:T(8,128)S(1)} custom-call(s32[128,4]{1,0:T(8,128)S(1)} %copy.14.tile_list, bf16[16,512,128]{2,1,0:T(8,128)(2,1)S(1)} %all_to_all.32.strip, bf16[8,2,128,512]{3,2,1,0:T(8,128)(2,1)S(1)} %bitcast.10, f32[1,128]{1,0:T(1,128)S(1)} %copy-done.4, s32[1,128]{1,0:T(1,128)S(1)} %copy-done.5), custom_call_target="tpu_custom_call" | custom-call | tf_op jit(solution)/shard_map/pallas_call | solution.py:227
  150.7 17.8 %all_to_all.33.arrived = f32[16,4,8,128]{3,2,1,0:T(8,128)S(1)} all-to-all(f32[16,4,8,128]{3,2,1,0:T(8,128)S(1)} %shard_map.72), channel_id=1, replica_groups=mesh['row'=8,'col'=16,'grid'=2] {'row','grid'}, dimensions={0} | all-to-all | bytes 524288 | tf_op jit(solution)/shard_map/all_to_all | solution.py:228
  168.5 1.3 shard_map.73.own
  169.9 0.0 collective-permute-start.1
  169.9 1.4 collective-permute-done.1.other
  171.3 0.0 copy-start.2
  171.3 0.7 copy-done.2
  172.0 3.9 %shard_map.74 = bf16[16,512,128]{2,1,0:T(8,128)(2,1)S(1)} custom-call(s32[128,4]{1,0:T(8,128)S(1)} %copy.14.tile_list, f32[4,8,128]{2,1,0:T(8,128)S(1)} %copy-done.2, f32[4,8,128]{2,1,0:T(8,128)S(1)} %collective-permute-done.1.other, bf16[8,2,128,512]{3,2,1,0:T(8,128)(2,1)S(1)} %bitcast.11), custom_call_target="tpu_custom_call" | custom-call | tf_op jit(solution)/shard_map/pallas_call | solution.py:233
  175.9 30.0 %all_to_all.34.pieces = bf16[16,512,128]{2,1,0:T(8,128)(2,1)S(1)} all-to-all(bf16[16,512,128]{2,1,0:T(8,128)(2,1)S(1)} %shard_map.74), channel_id=1, replica_groups=mesh['row'=8,'col'=16,'grid'=2] {'col'}, dimensions={0} | all-to-all | bytes 4194304 | tf_op jit(solution)/shard_map/all_to_all | solution.py:233
  205.9 0.9 shard_map.75
Async XLA Ops:
  7.2 46.5 %all-gather.2.cloned.1.call-start = ((), (), s32[]{:S(2)}) async-start(), calls=%async_computation.6 | async-start | bytes 2228224 | tf_op jit(solution)/shard_map/all_gather | solution.py:164
  10.5 7.7 %copy-start.7 = (s32[128,4]{0,1:T(4,128)S(1)}, s32[128,4]{0,1:T(4,128)}, u32[]{:S(2)}) copy-start(s32[128,4]{0,1:T(4,128)} %param.9) | copy-start | bytes 6148
  10.5 43.1 %copy-start.4 = (f32[1,128]{1,0:T(1,128)S(1)}, f32[1,128]{1,0:T(1,128)}, u32[]{:S(2)}) copy-start(f32[1,128]{1,0:T(1,128)} %weight.3) | copy-start | bytes 1540
  10.5 43.1 %copy-start.5 = (s32[1,128]{1,0:T(1,128)S(1)}, s32[1,128]{1,0:T(1,128)}, u32[]{:S(2)}) copy-start(s32[1,128]{1,0:T(1,128)} %screen.3) | copy-start | bytes 1540
  10.5 35.6 %all-to-all-start = ((bf16[16,512,128]{2,1,0:T(8,128)(2,1)}), bf16[16,512,128]{2,1,0:T(8,128)(2,1)S(1)}, u32[]{:S(2)}, u32[]{:S(2)}) async-start(bf16[16,512,128]{2,1,0:T(8,128)(2,1)} %broadcast_in_dim.8), calls=%async_computation | async-start | bytes 4194304 | tf_op jit(solution)/shard_map/all_to_all | solution.py:225
  46.1 7.5 %copy-start.6 = (bf16[16,512,128]{2,1,0:T(8,128)(2,1)}, bf16[16,512,128]{2,1,0:T(8,128)(2,1)S(1)}, u32[]{:S(2)}) copy-start(bf16[16,512,128]{2,1,0:T(8,128)(2,1)S(1)} %all-to-all-done.strip_far) | copy-start | bytes 6291460
  53.6 26.7 %copy-start = (bf16[16,128,512]{2,1,0:T(8,128)(2,1)S(1)}, bf16[16,128,512]{2,1,0:T(8,128)(2,1)}, u32[]{:S(2)}) copy-start(bf16[16,128,512]{2,1,0:T(8,128)(2,1)} %all-gather.2.cloned.1.call-done) | copy-start | bytes 6291460
  78.9 1.4 collective-permute-start
  80.3 0.7 copy-start.3
  85.0 32.4 %copy-start.1 = (bf16[2,1,4,64,128]{4,3,2,1,0:T(8,128)(2,1)S(1)}, bf16[2,1,4,64,128]{4,3,2,1,0:T(8,128)(2,1)}, u32[]{:S(2)}) copy-start(bf16[2,1,4,64,128]{4,3,2,1,0:T(8,128)(2,1)} %param.5) | copy-start | bytes 393220
  169.9 1.4 collective-permute-start.1
  171.3 0.7 copy-start.2
Sparse Core Ops, SparseCore 0:
  9.8 43.7 all-gather.1

commit v4 on v3

v4 whole, which is shorter than its diff:
```python
import functools

import jax
import jax.numpy as jnp
from jax import lax
from jax.experimental import pallas as pl
from jax.experimental.pallas import tpu as pltpu
from jax.sharding import PartitionSpec as P

MIXING = 0.001
VMEM_BYTES = 32 * 1024 * 1024


def everyone(x, n):
    return jnp.broadcast_to(x[None], (n, *x.shape))


def owned_multiple(row, tile, n_row, where=jnp.where, div=lax.div, rem=lax.rem):
    high = div(tile, n_row)
    return where(row <= rem(tile, n_row), high, 1 - high)


def partner(row, col, n_row):
    plain = dict(where=lambda a, b, c: b if a else c, div=lambda a, b: a // b, rem=lambda a, b: a % b)
    return col % n_row, owned_multiple(row, col, n_row, **plain) * n_row + row


def exchanges(n_row, n_col, n_grid, back):
    pairs = []
    for row in range(n_row):
        for col in range(n_col):
            to_row, to_col = partner(row, col, n_row)
            for core in range(n_grid):
                here = (row * n_col + col) * n_grid + core
                there = (to_row * n_col + to_col) * n_grid + core
                pairs.append((there, here) if back else (here, there))
    return pairs


def swapped(x):
    n = x.shape[1]
    rows = lax.broadcasted_iota(jnp.int32, (n, n), 0)
    lanes = lax.broadcasted_iota(jnp.int32, (n, n), 1)
    unit = jnp.where(rows == lanes, 1.0, 0.0).astype(jnp.bfloat16)
    return lax.dot_general(unit, x, (((1,), (1,)), ((), ())), preferred_element_type=jnp.float32)


def turn(tile, turned):
    width = tile.shape[1]
    for pair in range(turned.shape[0]):
        turned[pair] = swapped(tile[pair * width : (pair + 1) * width, :]).astype(jnp.bfloat16)


def joined(own, other, half):
    pairs, width = own.shape[:2]
    rows = pl.ds(pl.multiple_of(half * (width // 2), width // 2), width // 2)
    left = lax.broadcasted_iota(jnp.int32, (width // 2, width), 1) < width // 2
    comps = []
    for pair in range(pairs):
        mine = own[pair, rows, :].astype(jnp.float32)
        theirs = other[pair, rows, :].astype(jnp.float32)
        low = jnp.where(half == 0, mine, theirs)
        high = jnp.where(half == 0, theirs, mine)
        comps.append(jnp.where(left, low, pltpu.roll(high, width // 2, 1)))
        comps.append(jnp.where(left, pltpu.roll(low, width // 2, 1), high))
    return jnp.concatenate(comps, axis=0)


def find(tile_list, batch, n_row, my_row):
    columns = [tile_list[batch, s] for s in range(tile_list.shape[1])]
    slot = jnp.int32(0)
    multiple = jnp.int32(0)
    present = jnp.bool_(False)
    for s, tile in enumerate(columns):
        match = lax.rem(tile, n_row) == my_row
        slot = jnp.where(match, s, slot)
        multiple = jnp.where(match, lax.div(tile, n_row), multiple)
        present = jnp.logical_or(present, match)
    owned = [jnp.logical_and(present, owned_multiple(my_row, tile, n_row) == multiple) for tile in columns]
    return columns, slot, multiple, present, owned


def own_rows(basis, batch, slot, half, tile_width, half_tile):
    points = basis.shape[1] * basis.shape[2]
    block = basis[batch, :, :, pl.ds(pl.multiple_of(slot * tile_width, tile_width), tile_width)]
    block = block.reshape(points, tile_width)
    rows = lax.broadcasted_iota(jnp.int32, (half_tile, tile_width), 0) + half * half_tile
    lanes = lax.broadcasted_iota(jnp.int32, (half_tile, tile_width), 1)
    chosen = jnp.where(rows == lanes, 1.0, 0.0).astype(jnp.bfloat16)
    return lax.dot_general(chosen, block, (((1,), (1,)), ((), ())), preferred_element_type=jnp.float32)


def turn_kernel(density, turned, *, n_row, span):
    my_row = lax.axis_index("row")
    my_col = lax.axis_index("col")
    other = 1 - owned_multiple(my_row, my_col, n_row)
    turn(density[pl.ds(pl.multiple_of(other * span, span), span), :], turned)


def symmetric_kernel(density, mine, theirs, total, copies, *, n_row, span):
    my_row = lax.axis_index("row")
    my_col = lax.axis_index("col")
    half = lax.axis_index("grid")
    own = owned_multiple(my_row, my_col, n_row)
    tile = density[pl.ds(pl.multiple_of(own * span, span), span), :].astype(jnp.float32)
    mirror = joined(mine, theirs, half)
    tile = tile + jnp.where(lax.rem(my_col, n_row) == my_row, 0.0, mirror)
    total[...] = tile
    rounded = tile.astype(jnp.bfloat16)
    for dest in range(copies.shape[0]):
        copies[dest] = rounded


def add_densities(tile_list, strip, basis, arrival, weight, screen, out, sums, *, n_col, comps, half_tile, width):
    my_row = lax.axis_index("row")
    my_col = lax.axis_index("col")
    half = lax.axis_index("grid")
    n_row, n_half, half_points, functions = basis.shape
    nothing = jnp.zeros(strip.shape[1:], strip.dtype)
    for batch in range(n_row):
        columns, slot, multiple, present, owned = find(tile_list, batch * n_col + my_col, n_row, my_row)
        block = jnp.concatenate(
            [jnp.where(mine, strip[tile], nothing) for tile, mine in zip(columns, owned)], axis=1
        )
        arrival(batch)
        samples = basis[batch].reshape(n_half * half_points, functions)
        part = lax.dot_general(block, samples, (((1,), (1,)), ((), ())), preferred_element_type=jnp.float32)
        rows = own_rows(basis, batch, slot, half, width, half_tile)
        for comp in range(comps):
            piece = part[comp * half_tile : (comp + 1) * half_tile, :] * rows
            sums[comp, batch : batch + 1, :] = jnp.sum(piece, axis=0, keepdims=True)
    own = weight[...] * screen[...].astype(jnp.float32)
    for dest in range(out.shape[0]):
        h = dest % n_half
        out[dest, 0:comps] = sums[:, :, h * half_points : (h + 1) * half_points]
        if out.shape[1] > comps:
            out[dest, comps] = jnp.broadcast_to(own, out.shape[2:])


def first_density_kernel(tile_list, strip, basis_far, weight, screen, out, basis, sums, sems, **sizes):
    groups = sems.shape[0]
    size = basis.shape[0] // groups
    copies = [
        pltpu.make_async_copy(basis_far.at[pl.ds(g * size, size)], basis.at[pl.ds(g * size, size)], sems.at[g])
        for g in range(groups)
    ]
    for copy in copies:
        copy.start()

    def arrival(batch):
        if batch % size == 0:
            copies[batch // size].wait()

    add_densities(tile_list, strip, basis, arrival, weight, screen, out, sums, **sizes)


def density_kernel(tile_list, strip, basis, weight, screen, out, sums, **sizes):
    add_densities(tile_list, strip, basis, lambda batch: None, weight, screen, out, sums, **sizes)


def scales_of(dens, weights):
    total = dens[0]
    spin = [dens[comp] for comp in range(1, dens.shape[0])]
    norm = jnp.sqrt(1.0 + sum(s * s for s in spin))
    potentials = [total / jnp.sqrt(1.0 + total * total)] + [s / norm for s in spin]
    return [potential * weights for potential in potentials]


def first_scale_kernel(arrived, scales, weights):
    comps = scales.shape[0]
    n_row = weights.shape[0]
    half = lax.axis_index("grid")
    n_half = arrived.shape[0] // n_row
    for q in range(n_row):
        weights[q : q + 1, :] = arrived[q * n_half + half, comps, 0:1, :]
    for comp, scale in enumerate(scales_of(jnp.sum(arrived[:, 0:comps], axis=0), weights[...])):
        scales[comp] = scale


def scale_kernel(arrived, weights, scales):
    for comp, scale in enumerate(scales_of(jnp.sum(arrived[...], axis=0), weights[...])):
        scales[comp] = scale


def potential_kernel(tile_list, own, other, basis, out, scales, acc, seen, *, n_col, comps, half_tile, width):
    my_row = lax.axis_index("row")
    my_col = lax.axis_index("col")
    half = lax.axis_index("grid")
    n_row, n_half, half_points, functions = basis.shape
    multiples = out.shape[1]
    for tile in range(acc.shape[0]):
        for m in range(multiples):
            seen[tile, m] = 0
    scales[:, :, pl.ds(pl.multiple_of(half * half_points, half_points), half_points)] = own[...]
    scales[:, :, pl.ds(pl.multiple_of((1 - half) * half_points, half_points), half_points)] = other[...]
    for batch in range(n_row):
        columns, slot, multiple, present, owned = find(tile_list, batch * n_col + my_col, n_row, my_row)
        samples = basis[batch].reshape(n_half * half_points, functions)
        rows = own_rows(basis, batch, slot, half, width, half_tile)
        weighted = jnp.concatenate(
            [(rows * scales[comp, batch : batch + 1, :]).astype(jnp.bfloat16) for comp in range(comps)], axis=0
        )
        part = jnp.dot(weighted, samples, preferred_element_type=jnp.float32)
        m = 0 if multiples == 1 else multiple
        for s, tile in enumerate(columns):
            mine = owned[s] if multiples == 1 else present
            before = jnp.where(seen[tile, m] > 0, acc[tile, m], 0.0)
            acc[tile, m] = before + jnp.where(mine, part[:, s * width : (s + 1) * width], 0.0)
            seen[tile, m] = 1
    for tile in range(acc.shape[0]):
        for m in range(multiples):
            out[tile, m] = jnp.where(seen[tile, m] > 0, acc[tile, m], 0.0).astype(jnp.bfloat16)


def update_kernel(pieces, density, first, turned, copies, *, n_row):
    my_row = lax.axis_index("row")
    my_col = lax.axis_index("col")
    total = jnp.sum(pieces[...].astype(jnp.float32), axis=(0, 1)).astype(jnp.bfloat16)
    first[...] = total
    mixing = jnp.where(lax.rem(my_col, n_row) == my_row, MIXING, 2.0 * MIXING)
    updated = (density[...] + mixing * total.astype(jnp.float32)).astype(jnp.bfloat16)
    for dest in range(copies.shape[0]):
        copies[dest] = updated
    turn(total, turned)


def finish_kernel(pieces, first, mine, theirs, first_out, second_out, *, n_row):
    my_row = lax.axis_index("row")
    my_col = lax.axis_index("col")
    half = lax.axis_index("grid")
    own = owned_multiple(my_row, my_col, n_row)
    unpaired = lax.rem(my_col, n_row) == my_row
    second_out[...] = jnp.sum(pieces[...].astype(jnp.float32), axis=0).astype(jnp.bfloat16)
    first_out[own] = first[...]
    first_out[1 - own] = jnp.where(unpaired, 0.0, joined(mine, theirs, half)).astype(jnp.bfloat16)


def body(density, basis_values, quad_weight, screen, tile_list):
    n_row = lax.axis_size("row")
    n_col = lax.axis_size("col")
    n_grid = lax.axis_size("grid")
    row_tiles, _, comps, half_tile, width = density.shape
    half_points, functions = basis_values.shape[1:]
    points = half_points * n_grid
    rows = row_tiles * comps * half_tile
    span = comps * half_tile
    sizes = dict(n_col=n_col, comps=comps, half_tile=half_tile, width=width)
    own = density.reshape(rows, width)
    everywhere = ("row", "col", "grid")
    bf16 = lambda *shape: jax.ShapeDtypeStruct(shape, jnp.bfloat16)
    f32 = lambda *shape: jax.ShapeDtypeStruct(shape, jnp.float32)
    params = pltpu.CompilerParams(vmem_limit_bytes=VMEM_BYTES)
    smem = pl.BlockSpec(memory_space=pltpu.SMEM)
    hbm = pl.BlockSpec(memory_space=pltpu.HBM)
    vmem = pl.BlockSpec(memory_space=pltpu.VMEM)
    near = lambda x: pltpu.with_memory_space_constraint(x, pltpu.VMEM)

    def call(kernel, ins, outs, scratch=(), **settings):
        return pl.pallas_call(
            functools.partial(kernel, **settings),
            in_specs=ins,
            out_specs=[vmem] * len(outs),
            out_shape=outs,
            scratch_shapes=list(scratch),
            compiler_params=params,
        )

    block = (comps // n_grid, width, width)
    swap = [(0, 1), (1, 0)]
    sums = pltpu.VMEM((comps, n_row, points), jnp.float32)
    basis_shape = (n_row, n_grid, half_points, functions)
    basis_far = lax.all_gather(basis_values, ("row", "grid"), axis=0, tiled=True).reshape(basis_shape)

    def exchange(turned, back):
        mine = lax.ppermute(turned, everywhere, exchanges(n_row, n_col, n_grid, back))
        return mine, lax.ppermute(mine, "grid", swap)

    [turned] = call(turn_kernel, [vmem], [bf16(*block)], n_row=n_row, span=span)(own)
    symmetric, copies = call(
        symmetric_kernel, [vmem] * 3, [f32(span, width), bf16(n_col, span, width)], n_row=n_row, span=span
    )(own, *exchange(turned, True))

    def summed(partial):
        return near(lax.all_to_all(partial, ("row", "grid"), 0, 0, tiled=True))

    def slabs(mine, basis, multiples):
        other = lax.ppermute(mine, "grid", swap)
        shape = (n_col, multiples, span, width)
        [slab] = call(
            potential_kernel,
            [smem, vmem, vmem, vmem],
            [bf16(*shape)],
            [sums, pltpu.VMEM(shape, jnp.float32), pltpu.SMEM(shape[:2], jnp.int32)],
            **sizes,
        )(tile_list, near(mine), other, basis)
        return lax.all_to_all(slab, "col", 0, 0, tiled=True)

    message = (n_row * n_grid, comps, n_row, half_points)
    strip = near(lax.all_to_all(copies, "col", 0, 0, tiled=True))
    partial, basis = call(
        first_density_kernel,
        [smem, vmem, hbm, vmem, vmem],
        [f32(message[0], comps + 1, *message[2:]), bf16(*basis_shape)],
        [sums, pltpu.SemaphoreType.DMA((2,))],
        **sizes,
    )(tile_list, strip, pltpu.with_memory_space_constraint(basis_far, pltpu.HBM), quad_weight, screen)
    basis = near(basis)
    mine, weights = call(first_scale_kernel, [vmem], [f32(*message[1:]), f32(*message[2:])])(summed(partial))
    first, turned, copies = call(
        update_kernel, [vmem] * 2, [bf16(span, width), bf16(*block), bf16(n_col, span, width)], n_row=n_row
    )(slabs(mine, basis, 1), symmetric)
    mirrors = exchange(turned, False)
    strip = near(lax.all_to_all(copies, "col", 0, 0, tiled=True))
    [partial] = call(density_kernel, [smem] + [vmem] * 4, [f32(*message)], [sums], **sizes)(
        tile_list, strip, basis, quad_weight, screen
    )
    [mine] = call(scale_kernel, [vmem] * 2, [f32(*message[1:])])(summed(partial), near(weights))
    outs = call(finish_kernel, [vmem] * 4, [bf16(row_tiles, span, width)] * 2, n_row=n_row)(
        slabs(mine, basis, row_tiles), first, *mirrors
    )
    return tuple(out.reshape(density.shape) for out in outs)


def solution(mesh):
    in_specs = (
        P(None, "row", None, "grid", "col"),
        P(("row", "col"), "grid", None),
        P(("row", "col"), "grid"),
        P(("row", "col"), "grid"),
        P(),
    )
    out_specs = (P(None, "row", None, "grid", "col"), P(None, "row", None, "grid", "col"))
    return jax.shard_map(body, mesh=mesh, in_specs=in_specs, out_specs=out_specs, check_vma=False)
```

time: 214 us -> 191 us (0.89)
  blocking collectives: 129 us -> 75.8 us
  starting transfers between devices: 7.76 us -> 26.8 us
  waiting for transfers between devices: 38.7 us -> 53.9 us
  Pallas kernels: 20.4 us -> 17 us
    all_to_all x5 -> x4, blocking collectives: 129 us -> 75.8 us  [the longest x2 38.6 us: summed(): return near(lax.all_to_all(partial, ('row', 'grid'), 0, 0, tiled=True))]
    all_to_all x1 -> x2, waiting for transfers between devices: 27.8 us -> 44.7 us  [the longest x1 29.1 us: slabs(): return lax.all_to_all(slab, 'col', 0, 0, tiled=True)]
    all_to_all x1 -> x2, starting transfers between devices: 7.72 us -> 21.7 us  [the longest x1 18 us: body(): strip = near(lax.all_to_all(copies, 'col', 0, 0, tiled=True))]
    ppermute x2 -> x6, starting transfers between devices: 0.01 us -> 5.11 us  [the longest x2 3.6 us: exchange(): return (mine, lax.ppermute(mine, 'grid', swap))]
    pallas_call x8 -> x10, Pallas kernels: 20.4 us -> 17 us  [the longest x2 7.42 us: slabs(): call(potential_kernel, [smem, vmem, vmem, vmem], [bf16(*shape)], [sums, p...]
    all_gather x1, waiting for transfers between devices: 7.49 us -> 4.18 us  [body(): lax.all_gather(basis_values, ('row', 'grid'), axis=0, tiled=True)]
    broadcast_in_dim x1 -> x0, local copies, waits for them, and re-layouts: 2.64 us -> none  [everyone(): return jnp.broadcast_to(x[None], (n, *x.shape))]
    ppermute x2 -> x6, waiting for transfers between devices: 2.78 us -> 4.32 us  [the longest x2 2.34 us: slabs(): other = lax.ppermute(mine, 'grid', swap)]
  transfers between devices with their start and end apart: 4 -> 9, of which waited for: 4 -> 7; matrix products, arithmetic and copies ran while one was open for 1% -> 0% of each run, Pallas kernels for 0% -> 1%
where the time goes in v4:
time: 191 us
  blocking collectives  75.8 us (40%)
  waiting for transfers between devices  53.9 us (28%)
  starting transfers between devices  26.8 us (14%)
  Pallas kernels  17 us (9%)
  between operations  14.2 us (7%)
  local copies, waits for them, and re-layouts  3.25 us (2%)
    all_to_all x2, blocking collectives, summed(): return near(lax.all_to_all(partial, ('row', 'grid'), 0, 0, tiled=True))  38.6 us
    all_to_all x1, waiting for transfers between devices, slabs(): return lax.all_to_all(slab, 'col', 0, 0, tiled=True)  29.1 us
    all_to_all x1, blocking collectives, slabs(): return lax.all_to_all(slab, 'col', 0, 0, tiled=True)  18.8 us
    all_to_all x1, blocking collectives, body(): strip = near(lax.all_to_all(copies, 'col', 0, 0, tiled=True))  18.5 us
    all_to_all x1, starting transfers between devices, body(): strip = near(lax.all_to_all(copies, 'col', 0, 0, tiled=True))  18 us
    all_to_all x1, waiting for transfers between devices, body(): strip = near(lax.all_to_all(copies, 'col', 0, 0, tiled=True))  15.5 us
    pallas_call x2, Pallas kernels, slabs(): call(potential_kernel, [smem, vmem, vmem, vmem], [bf16(*shape)], [sums, p...  7.42 us
    all_gather x1, waiting for transfers between devices, body(): lax.all_gather(basis_values, ('row', 'grid'), axis=0, tiled=True)  4.18 us
  transfers between devices with their start and end apart: 9, of which 7 were waited for; matrix products, arithmetic and copies ran while one was open for 0% of the time, Pallas kernels for 1%

profile of v4, /device:TPU:1, one launch (start us, length us, event | category | flops | bytes accessed | tf_op | source)
XLA Modules:
  0.0 190.9 jit_solution(10867982605947774132)
XLA Ops:
  7.2 0.0 copy-start.5
  7.2 0.0 copy-start.4
  7.2 0.0 copy-start.3
  7.2 0.0 all-gather.2.cloned.1.call-start
  7.2 0.7 all-gather.2.cloned.1.call-update
  7.9 0.0 copy-start.1
  7.9 0.9 copy-done.1
  8.8 0.2 shard_map.68
  9.0 0.7 collective-permute-start
  9.7 0.0 collective-permute-done.mine
  9.7 3.3 %collective-permute-start.1 = (bf16[2,128,128]{2,1,0:T(8,128)(2,1)S(1)}, bf16[2,128,128]{2,1,0:T(8,128)(2,1)S(1)}, u32[]{:S(2)}, u32[]{:S(2)}) collective-permute-start(bf16[2,128,128]{2,1,0:T(8,128)(2,1)S(1)} %collective-permute-done.mine), channel_id=1, source_target_pairs={{0,1},{1,0},{2,3},{3,2},{4,5},{5,4},{6,7},{7,6},{8,9},{9,8},{10,11... | collective-permute-start | bytes 196616 | tf_op jit(solution)/shard_map/ppermute | solution.py:276
  13.0 0.9 collective-permute-done.1.theirs
  13.9 0.0 copy-start.2
  13.9 0.9 copy-done.2
  14.8 1.2 shard_map.69
  16.0 18.0 %all-to-all-start = ((bf16[16,256,128]{2,1,0:T(8,128)(2,1)}), bf16[16,256,128]{2,1,0:T(8,128)(2,1)S(1)}, u32[]{:S(2)}, u32[]{:S(2)}) async-start(bf16[16,256,128]{2,1,0:T(8,128)(2,1)} %get-tuple-element.13), calls=%async_computation | async-start | bytes 2097152 | tf_op jit(solution)/shard_map/all_to_all | solution.py:299
  34.0 0.0 copy-done.5
  34.0 0.1 copy.16.tile_list
  34.1 15.5 %all-to-all-done.strip = bf16[16,256,128]{2,1,0:T(8,128)(2,1)S(1)} async-done(((bf16[16,256,128]{2,1,0:T(8,128)(2,1)}), bf16[16,256,128]{2,1,0:T(8,128)(2,1)S(1)}, u32[]{:S(2)}, u32[]{:S(2)}) %all-to-all-start) | async-done | bytes 1048608 | tf_op jit(solution)/shard_map/all_to_all | solution.py:299
  49.7 4.2 %all-gather.2.cloned.1.call-done = bf16[16,128,512]{2,1,0:T(8,128)(2,1)} async-done(((bf16[1,128,512]{2,1,0:T(8,128)(2,1)}), bf16[16,128,512]{2,1,0:T(8,128)(2,1)}) %all-gather.2.cloned.1.call-update) | async-done | bytes 2097168 | tf_op jit(solution)/shard_map/all_gather | solution.py:272
  53.8 0.0 copy-done.4
  53.8 0.0 copy-done.3
  53.8 4.1 %shard_map.70 = (f32[16,5,8,128]{3,2,1,0:T(8,128)S(1)}, bf16[8,2,128,512]{3,2,1,0:T(8,128)(2,1)S(1)}) custom-call(s32[128,4]{1,0:T(8,128)S(1)} %copy.16.tile_list, bf16[16,256,128]{2,1,0:T(8,128)(2,1)S(1)} %all-to-all-done.strip, bf16[8,2,128,512]{3,2,1,0:T(8,128)(2,1)} %bitcast.10, f32[1,128]{1,0:T(1,128)S(1)} %copy-done.3, s32[1,128]{1,0:T(1,128)S(1)} %copy-done.4), custom_call_target="tpu_custom_call" | custom-call | tf_op jit(solution)/shard_map/pallas_call | solution.py:300
  57.9 20.7 %all_to_all.30.arrived = f32[16,5,8,128]{3,2,1,0:T(8,128)S(1)} all-to-all(f32[16,5,8,128]{3,2,1,0:T(8,128)S(1)} %get-tuple-element.14), channel_id=1, replica_groups=mesh['row'=8,'col'=16,'grid'=2] {'row','grid'}, dimensions={0} | all-to-all | bytes 655360 | tf_op jit(solution)/shard_map/all_to_all | solution.py:284
  78.7 0.1 collective-permute-start.2
  78.8 1.2 collective-permute-done.2.other
  80.0 3.6 %shard_map.72 = bf16[16,1,256,128]{3,2,1,0:T(8,128)(2,1)S(1)} custom-call(s32[128,4]{1,0:T(8,128)S(1)} %copy.16.tile_list, f32[4,8,128]{2,1,0:T(8,128)S(1)} %get-tuple-element.15.own, f32[4,8,128]{2,1,0:T(8,128)S(1)} %collective-permute-done.2.other, bf16[8,2,128,512]{3,2,1,0:T(8,128)(2,1)S(1)} %get-tuple-element.16.basis), custom_call_target="tpu_custom_call" | custom-call | tf_op jit(solution)/shard_map/pallas_call | solution.py:289
  83.6 18.8 %all_to_all.31.pieces = bf16[16,1,256,128]{3,2,1,0:T(8,128)(2,1)S(1)} all-to-all(bf16[16,1,256,128]{3,2,1,0:T(8,128)(2,1)S(1)} %shard_map.72), channel_id=1, replica_groups=mesh['row'=8,'col'=16,'grid'=2] {'col'}, dimensions={0} | all-to-all | bytes 2097152 | tf_op jit(solution)/shard_map/all_to_all | solution.py:296
  102.4 0.3 shard_map.73
  102.8 18.5 %all_to_all.32.strip = bf16[16,256,128]{2,1,0:T(8,128)(2,1)S(1)} all-to-all(bf16[16,256,128]{2,1,0:T(8,128)(2,1)S(1)} %get-tuple-element.18), channel_id=1, replica_groups=mesh['row'=8,'col'=16,'grid'=2] {'col'}, dimensions={0} | all-to-all | bytes 2097152 | tf_op jit(solution)/shard_map/all_to_all | solution.py:313
  121.2 2.6 %shard_map.74 = f32[16,4,8,128]{3,2,1,0:T(8,128)S(1)} custom-call(s32[128,4]{1,0:T(8,128)S(1)} %copy.16.tile_list, bf16[16,256,128]{2,1,0:T(8,128)(2,1)S(1)} %all_to_all.32.strip, bf16[8,2,128,512]{3,2,1,0:T(8,128)(2,1)S(1)} %get-tuple-element.16.basis, f32[1,128]{1,0:T(1,128)S(1)} %copy-done.3, s32[1,128]{1,0:T(1,128)S(1)} %copy-done.4), custom_call_target="tpu_custom_call" | custom-call | tf_op jit(solution)/shard_map/pallas_call | solution.py:314
  123.8 17.8 %all_to_all.33.arrived = f32[16,4,8,128]{3,2,1,0:T(8,128)S(1)} all-to-all(f32[16,4,8,128]{3,2,1,0:T(8,128)S(1)} %shard_map.74), channel_id=1, replica_groups=mesh['row'=8,'col'=16,'grid'=2] {'row','grid'}, dimensions={0} | all-to-all | bytes 524288 | tf_op jit(solution)/shard_map/all_to_all | solution.py:284
  141.7 0.1 collective-permute-start.3
  141.8 1.2 collective-permute-done.3.other
  143.0 3.8 %shard_map.76 = bf16[16,2,256,128]{3,2,1,0:T(8,128)(2,1)S(1)} custom-call(s32[128,4]{1,0:T(8,128)S(1)} %copy.16.tile_list, f32[4,8,128]{2,1,0:T(8,128)S(1)} %shard_map.75.own, f32[4,8,128]{2,1,0:T(8,128)S(1)} %collective-permute-done.3.other, bf16[8,2,128,512]{3,2,1,0:T(8,128)(2,1)S(1)} %get-tuple-element.16.basis), custom_call_target="tpu_custom_call" | custom-call | tf_op jit(solution)/shard_map/pallas_call | solution.py:289
  146.8 0.0 copy-start
  146.8 1.3 copy-done
  148.1 3.7 %all-to-all-start.5 = ((bf16[16,2,256,128]{3,2,1,0:T(8,128)(2,1)}), bf16[16,2,256,128]{3,2,1,0:T(8,128)(2,1)S(1)}, u32[]{:S(2)}, u32[]{:S(2)}) async-start(bf16[16,2,256,128]{3,2,1,0:T(8,128)(2,1)} %copy-done), calls=%async_computation.5 | async-start | bytes 4194304 | tf_op jit(solution)/shard_map/all_to_all | solution.py:296
  151.8 0.7 collective-permute-start.4
  152.5 0.0 collective-permute-done.4.mine
  152.5 0.3 collective-permute-start.5
  152.8 1.1 collective-permute-done.5.theirs
  153.8 29.1 %all-to-all-done.5.pieces = bf16[16,2,256,128]{3,2,1,0:T(8,128)(2,1)S(1)} async-done(((bf16[16,2,256,128]{3,2,1,0:T(8,128)(2,1)}), bf16[16,2,256,128]{3,2,1,0:T(8,128)(2,1)S(1)}, u32[]{:S(2)}, u32[]{:S(2)}) %all-to-all-start.5) | async-done | bytes 2097184 | tf_op jit(solution)/shard_map/all_to_all | solution.py:296
  183.0 1.1 shard_map.77
  (2 shorter events, 0.1 us)
Async XLA Ops:
  7.2 26.8 %copy-start.5 = (s32[128,4]{0,1:T(4,128)S(1)}, s32[128,4]{0,1:T(4,128)}, u32[]{:S(2)}) copy-start(s32[128,4]{0,1:T(4,128)} %param.9) | copy-start | bytes 6148
  7.2 46.7 %copy-start.4 = (s32[1,128]{1,0:T(1,128)S(1)}, s32[1,128]{1,0:T(1,128)}, u32[]{:S(2)}) copy-start(s32[1,128]{1,0:T(1,128)} %screen.3) | copy-start | bytes 1540
  7.2 46.7 %copy-start.3 = (f32[1,128]{1,0:T(1,128)S(1)}, f32[1,128]{1,0:T(1,128)}, u32[]{:S(2)}) copy-start(f32[1,128]{1,0:T(1,128)} %weight.3) | copy-start | bytes 1540
  7.2 46.6 %all-gather.2.cloned.1.call-start = ((), (), s32[]{:S(2)}) async-start(), calls=%async_computation.6 | async-start | bytes 2228224 | tf_op jit(solution)/shard_map/all_gather | solution.py:272
  7.9 0.9 copy-start.1
  9.0 0.7 collective-permute-start
  9.7 4.2 %collective-permute-start.1 = (bf16[2,128,128]{2,1,0:T(8,128)(2,1)S(1)}, bf16[2,128,128]{2,1,0:T(8,128)(2,1)S(1)}, u32[]{:S(2)}, u32[]{:S(2)}) collective-permute-start(bf16[2,128,128]{2,1,0:T(8,128)(2,1)S(1)} %collective-permute-done.mine), channel_id=1, source_target_pairs={{0,1},{1,0},{2,3},{3,2},{4,5},{5,4},{6,7},{7,6},{8,9},{9,8},{10,11... | collective-permute-start | bytes 196616 | tf_op jit(solution)/shard_map/ppermute | solution.py:276
  13.9 0.9 copy-start.2
  16.0 33.7 %all-to-all-start = ((bf16[16,256,128]{2,1,0:T(8,128)(2,1)}), bf16[16,256,128]{2,1,0:T(8,128)(2,1)S(1)}, u32[]{:S(2)}, u32[]{:S(2)}) async-start(bf16[16,256,128]{2,1,0:T(8,128)(2,1)} %get-tuple-element.13), calls=%async_computation | async-start | bytes 2097152 | tf_op jit(solution)/shard_map/all_to_all | solution.py:299
  78.7 1.3 collective-permute-start.2
  141.7 1.3 collective-permute-start.3
  146.8 1.3 copy-start
  148.1 34.9 %all-to-all-start.5 = ((bf16[16,2,256,128]{3,2,1,0:T(8,128)(2,1)}), bf16[16,2,256,128]{3,2,1,0:T(8,128)(2,1)S(1)}, u32[]{:S(2)}, u32[]{:S(2)}) async-start(bf16[16,2,256,128]{3,2,1,0:T(8,128)(2,1)} %copy-done), calls=%async_computation.5 | async-start | bytes 4194304 | tf_op jit(solution)/shard_map/all_to_all | solution.py:296
  151.8 0.7 collective-permute-start.4
  152.5 1.3 collective-permute-start.5
Sparse Core Ops, SparseCore 0:
  9.9 43.9 all-gather.1

commit v5 on v4

--- a/solution.py
+++ b/solution.py
@@ -66,8 +66,9 @@
     return jnp.concatenate(comps, axis=0)
 
 
-def find(tile_list, batch, n_row, my_row):
-    columns = [tile_list[batch, s] for s in range(tile_list.shape[1])]
+def find(tiles, batch, n_row, my_row):
+    count = tiles.shape[0] // n_row
+    columns = [tiles[batch * count + s] for s in range(count)]
     slot = jnp.int32(0)
     multiple = jnp.int32(0)
     present = jnp.bool_(False)
@@ -87,7 +88,9 @@
     rows = lax.broadcasted_iota(jnp.int32, (half_tile, tile_width), 0) + half * half_tile
     lanes = lax.broadcasted_iota(jnp.int32, (half_tile, tile_width), 1)
     chosen = jnp.where(rows == lanes, 1.0, 0.0).astype(jnp.bfloat16)
-    return lax.dot_general(chosen, block, (((1,), (1,)), ((), ())), preferred_element_type=jnp.float32)
+    return lax.dot_general(
+        chosen, block, (((1,), (1,)), ((), ())), preferred_element_type=jnp.float32
+    ).astype(jnp.bfloat16)
 
 
 def turn_kernel(density, turned, *, n_row, span):
@@ -111,21 +114,18 @@
         copies[dest] = rounded
 
 
-def add_densities(tile_list, strip, basis, arrival, weight, screen, out, sums, *, n_col, comps, half_tile, width):
-    my_row = lax.axis_index("row")
-    my_col = lax.axis_index("col")
-    half = lax.axis_index("grid")
+def add_densities(tiles, strip, basis, rows_of, weight, screen, out, sums, *, n_col, comps, half_tile, width):
+    my_row = lax.axis_index("row")
     n_row, n_half, half_points, functions = basis.shape
     nothing = jnp.zeros(strip.shape[1:], strip.dtype)
     for batch in range(n_row):
-        columns, slot, multiple, present, owned = find(tile_list, batch * n_col + my_col, n_row, my_row)
+        columns, slot, multiple, present, owned = find(tiles, batch, n_row, my_row)
         block = jnp.concatenate(
             [jnp.where(mine, strip[tile], nothing) for tile, mine in zip(columns, owned)], axis=1
         )
-        arrival(batch)
+        rows = rows_of(batch, slot).astype(jnp.float32)
         samples = basis[batch].reshape(n_half * half_points, functions)
         part = lax.dot_general(block, samples, (((1,), (1,)), ((), ())), preferred_element_type=jnp.float32)
-        rows = own_rows(basis, batch, slot, half, width, half_tile)
         for comp in range(comps):
             piece = part[comp * half_tile : (comp + 1) * half_tile, :] * rows
             sums[comp, batch : batch + 1, :] = jnp.sum(piece, axis=0, keepdims=True)
@@ -137,7 +137,8 @@
             out[dest, comps] = jnp.broadcast_to(own, out.shape[2:])
 
 
-def first_density_kernel(tile_list, strip, basis_far, weight, screen, out, basis, sums, sems, **sizes):
+def first_density_kernel(tiles, strip, basis_far, weight, screen, out, basis, rows, sums, sems, **sizes):
+    half = lax.axis_index("grid")
     groups = sems.shape[0]
     size = basis.shape[0] // groups
     copies = [
@@ -147,15 +148,17 @@
     for copy in copies:
         copy.start()
 
-    def arrival(batch):
+    def rows_of(batch, slot):
         if batch % size == 0:
             copies[batch // size].wait()
-
-    add_densities(tile_list, strip, basis, arrival, weight, screen, out, sums, **sizes)
-
-
-def density_kernel(tile_list, strip, basis, weight, screen, out, sums, **sizes):
-    add_densities(tile_list, strip, basis, lambda batch: None, weight, screen, out, sums, **sizes)
+        rows[batch] = own_rows(basis, batch, slot, half, sizes["width"], sizes["half_tile"])
+        return rows[batch]
+
+    add_densities(tiles, strip, basis, rows_of, weight, screen, out, sums, **sizes)
+
+
+def density_kernel(tiles, strip, basis, rows, weight, screen, out, sums, **sizes):
+    add_densities(tiles, strip, basis, lambda batch, slot: rows[batch], weight, screen, out, sums, **sizes)
 
 
 def scales_of(dens, weights):
@@ -182,34 +185,28 @@
         scales[comp] = scale
 
 
-def potential_kernel(tile_list, own, other, basis, out, scales, acc, seen, *, n_col, comps, half_tile, width):
-    my_row = lax.axis_index("row")
-    my_col = lax.axis_index("col")
+def potential_kernel(tiles, own, other, basis, rows, out, scales, acc, *, n_col, comps, half_tile, width):
+    my_row = lax.axis_index("row")
     half = lax.axis_index("grid")
     n_row, n_half, half_points, functions = basis.shape
     multiples = out.shape[1]
-    for tile in range(acc.shape[0]):
-        for m in range(multiples):
-            seen[tile, m] = 0
+    acc[...] = jnp.zeros_like(acc)
     scales[:, :, pl.ds(pl.multiple_of(half * half_points, half_points), half_points)] = own[...]
     scales[:, :, pl.ds(pl.multiple_of((1 - half) * half_points, half_points), half_points)] = other[...]
     for batch in range(n_row):
-        columns, slot, multiple, present, owned = find(tile_list, batch * n_col + my_col, n_row, my_row)
+        columns, slot, multiple, present, owned = find(tiles, batch, n_row, my_row)
         samples = basis[batch].reshape(n_half * half_points, functions)
-        rows = own_rows(basis, batch, slot, half, width, half_tile)
+        factor = rows[batch].astype(jnp.float32)
         weighted = jnp.concatenate(
-            [(rows * scales[comp, batch : batch + 1, :]).astype(jnp.bfloat16) for comp in range(comps)], axis=0
+            [(factor * scales[comp, batch : batch + 1, :]).astype(jnp.bfloat16) for comp in range(comps)], axis=0
         )
         part = jnp.dot(weighted, samples, preferred_element_type=jnp.float32)
         m = 0 if multiples == 1 else multiple
         for s, tile in enumerate(columns):
             mine = owned[s] if multiples == 1 else present
-            before = jnp.where(seen[tile, m] > 0, acc[tile, m], 0.0)
-            acc[tile, m] = before + jnp.where(mine, part[:, s * width : (s + 1) * width], 0.0)
-            seen[tile, m] = 1
-    for tile in range(acc.shape[0]):
-        for m in range(multiples):
-            out[tile, m] = jnp.where(seen[tile, m] > 0, acc[tile, m], 0.0).astype(jnp.bfloat16)
+            tile = jnp.where(mine, tile, n_col)
+            acc[tile, m] += part[:, s * width : (s + 1) * width]
+    out[...] = acc[0:n_col].astype(jnp.bfloat16)
 
 
 def update_kernel(pieces, density, first, turned, copies, *, n_row):
@@ -224,15 +221,18 @@
     turn(total, turned)
 
 
-def finish_kernel(pieces, first, mine, theirs, first_out, second_out, *, n_row):
+def mirror_kernel(first, mine, theirs, first_out, *, n_row):
     my_row = lax.axis_index("row")
     my_col = lax.axis_index("col")
     half = lax.axis_index("grid")
     own = owned_multiple(my_row, my_col, n_row)
     unpaired = lax.rem(my_col, n_row) == my_row
-    second_out[...] = jnp.sum(pieces[...].astype(jnp.float32), axis=0).astype(jnp.bfloat16)
     first_out[own] = first[...]
     first_out[1 - own] = jnp.where(unpaired, 0.0, joined(mine, theirs, half)).astype(jnp.bfloat16)
+
+
+def sum_kernel(pieces, out):
+    out[...] = jnp.sum(pieces[...].astype(jnp.float32), axis=0).astype(jnp.bfloat16)
 
 
 def body(density, basis_values, quad_weight, screen, tile_list):
@@ -275,6 +275,8 @@
         mine = lax.ppermute(turned, everywhere, exchanges(n_row, n_col, n_grid, back))
         return mine, lax.ppermute(mine, "grid", swap)
 
+    by_row = tile_list.reshape(n_row, n_col, tile_list.shape[1])
+    tiles = lax.dynamic_index_in_dim(by_row, lax.axis_index("col"), 1, keepdims=False).reshape(-1)
     [turned] = call(turn_kernel, [vmem], [bf16(*block)], n_row=n_row, span=span)(own)
     symmetric, copies = call(
         symmetric_kernel, [vmem] * 3, [f32(span, width), bf16(n_col, span, width)], n_row=n_row, span=span
@@ -288,36 +290,36 @@
         shape = (n_col, multiples, span, width)
         [slab] = call(
             potential_kernel,
-            [smem, vmem, vmem, vmem],
+            [smem] + [vmem] * 4,
             [bf16(*shape)],
-            [sums, pltpu.VMEM(shape, jnp.float32), pltpu.SMEM(shape[:2], jnp.int32)],
+            [sums, pltpu.VMEM((n_col + 1, *shape[1:]), jnp.float32)],
             **sizes,
-        )(tile_list, near(mine), other, basis)
+        )(tiles, near(mine), other, basis, kept_rows)
         return lax.all_to_all(slab, "col", 0, 0, tiled=True)
 
     message = (n_row * n_grid, comps, n_row, half_points)
     strip = near(lax.all_to_all(copies, "col", 0, 0, tiled=True))
-    partial, basis = call(
+    partial, basis, kept_rows = call(
         first_density_kernel,
         [smem, vmem, hbm, vmem, vmem],
-        [f32(message[0], comps + 1, *message[2:]), bf16(*basis_shape)],
+        [f32(message[0], comps + 1, *message[2:]), bf16(*basis_shape), bf16(n_row, half_tile, points)],
         [sums, pltpu.SemaphoreType.DMA((2,))],
         **sizes,
-    )(tile_list, strip, pltpu.with_memory_space_constraint(basis_far, pltpu.HBM), quad_weight, screen)
-    basis = near(basis)
+    )(tiles, strip, pltpu.with_memory_space_constraint(basis_far, pltpu.HBM), quad_weight, screen)
+    basis, kept_rows = near(basis), near(kept_rows)
     mine, weights = call(first_scale_kernel, [vmem], [f32(*message[1:]), f32(*message[2:])])(summed(partial))
     first, turned, copies = call(
         update_kernel, [vmem] * 2, [bf16(span, width), bf16(*block), bf16(n_col, span, width)], n_row=n_row
     )(slabs(mine, basis, 1), symmetric)
     mirrors = exchange(turned, False)
     strip = near(lax.all_to_all(copies, "col", 0, 0, tiled=True))
-    [partial] = call(density_kernel, [smem] + [vmem] * 4, [f32(*message)], [sums], **sizes)(
-        tile_list, strip, basis, quad_weight, screen
+    [partial] = call(density_kernel, [smem] + [vmem] * 5, [f32(*message)], [sums], **sizes)(
+        tiles, strip, basis, kept_rows, quad_weight, screen
     )
     [mine] = call(scale_kernel, [vmem] * 2, [f32(*message[1:])])(summed(partial), near(weights))
-    outs = call(finish_kernel, [vmem] * 4, [bf16(row_tiles, span, width)] * 2, n_row=n_row)(
-        slabs(mine, basis, row_tiles), first, *mirrors
-    )
+    whole = [bf16(row_tiles, span, width)]
+    outs = call(mirror_kernel, [vmem] * 3, whole, n_row=n_row)(first, *mirrors)
+    outs += call(sum_kernel, [vmem], whole)(slabs(mine, basis, row_tiles))
     return tuple(out.reshape(density.shape) for out in outs)
 
 

time: 191 us -> 185 us (0.969)
  Pallas kernels: 17 us -> 12.7 us
  local copies, waits for them, and re-layouts: 3.25 us -> 1.28 us
    pallas_call x4 -> x5, Pallas kernels: 11.2 us -> 7.99 us  [the longest x2 4.94 us: slabs(): call(potential_kernel, [smem] + [vmem] * 4, [bf16(*shape)], [sums, pltpu....]
    unnamed x13 -> x9, local copies, waits for them, and re-layouts: 3.25 us -> 1.05 us
where the time goes in v5:
time: 185 us; the launch traced here: 184 us
  blocking collectives  75.7 us (41%)
  waiting for transfers between devices  53.7 us (29%)
  starting transfers between devices  26.8 us (14%)
  between operations  14.2 us (8%)
  Pallas kernels  12.7 us (7%)
    all_to_all x2, blocking collectives, summed(): return near(lax.all_to_all(partial, ('row', 'grid'), 0, 0, tiled=True))  37.8 us
    all_to_all x1, waiting for transfers between devices, slabs(): return lax.all_to_all(slab, 'col', 0, 0, tiled=True)  28.5 us
    all_to_all x1, blocking collectives, slabs(): return lax.all_to_all(slab, 'col', 0, 0, tiled=True)  19.5 us
    all_to_all x1, blocking collectives, body(): strip = near(lax.all_to_all(copies, 'col', 0, 0, tiled=True))  18.5 us
    all_to_all x1, starting transfers between devices, body(): strip = near(lax.all_to_all(copies, 'col', 0, 0, tiled=True))  18 us
    all_to_all x1, waiting for transfers between devices, body(): strip = near(lax.all_to_all(copies, 'col', 0, 0, tiled=True))  15.3 us
    pallas_call x2, Pallas kernels, slabs(): call(potential_kernel, [smem] + [vmem] * 4, [bf16(*shape)], [sums, pltpu....  4.94 us
    all_gather x1, waiting for transfers between devices, body(): lax.all_gather(basis_values, ('row', 'grid'), axis=0, tiled=True)  4.92 us
  transfers between devices with their start and end apart: 9, of which 7 were waited for; matrix products, arithmetic and copies ran while one was open for 0% of the time, Pallas kernels for 1%

profile of v5, /device:TPU:1, one launch (start us, length us, event | category | flops | bytes accessed | tf_op | source)
XLA Modules:
  0.0 184.5 jit_solution(11747471466414831621)
XLA Ops:
  7.2 0.0 copy-start.3
  7.2 0.0 copy-start.2
  7.2 0.0 copy-start.1
  7.2 0.0 all-gather.2.cloned.1.call-start
  7.2 0.7 all-gather.2.cloned.1.call-update
  7.9 0.0 copy-start
  7.9 0.9 copy-done
  8.8 0.2 shard_map.68
  9.0 0.7 collective-permute-start
  9.7 0.0 collective-permute-done.mine
  9.7 3.3 %collective-permute-start.1 = (bf16[2,128,128]{2,1,0:T(8,128)(2,1)S(1)}, bf16[2,128,128]{2,1,0:T(8,128)(2,1)S(1)}, u32[]{:S(2)}, u32[]{:S(2)}) collective-permute-start(bf16[2,128,128]{2,1,0:T(8,128)(2,1)S(1)} %collective-permute-done.mine), channel_id=1, source_target_pairs={{0,1},{1,0},{2,3},{3,2},{4,5},{5,4},{6,7},{7,6},{8,9},{9,8},{10,11... | collective-permute-start | bytes 196616 | tf_op jit(solution)/shard_map/ppermute | solution.py:276
  13.0 0.9 collective-permute-done.1.theirs
  13.9 1.2 shard_map.69
  15.1 18.0 %all-to-all-start = ((bf16[16,256,128]{2,1,0:T(8,128)(2,1)}), bf16[16,256,128]{2,1,0:T(8,128)(2,1)S(1)}, u32[]{:S(2)}, u32[]{:S(2)}) async-start(bf16[16,256,128]{2,1,0:T(8,128)(2,1)} %get-tuple-element.12), calls=%async_computation | async-start | bytes 2097152 | tf_op jit(solution)/shard_map/all_to_all | solution.py:301
  33.1 0.0 copy-done.3
  33.1 0.1 reshape.23
  33.2 0.1 constant_dynamic-slice_fusion
  33.3 0.1 copy.16
  33.4 0.1 reshape.24.tiles
  33.5 15.3 %all-to-all-done.strip = bf16[16,256,128]{2,1,0:T(8,128)(2,1)S(1)} async-done(((bf16[16,256,128]{2,1,0:T(8,128)(2,1)}), bf16[16,256,128]{2,1,0:T(8,128)(2,1)S(1)}, u32[]{:S(2)}, u32[]{:S(2)}) %all-to-all-start) | async-done | bytes 1048608 | tf_op jit(solution)/shard_map/all_to_all | solution.py:301
  48.8 4.9 %all-gather.2.cloned.1.call-done = bf16[16,128,512]{2,1,0:T(8,128)(2,1)} async-done(((bf16[1,128,512]{2,1,0:T(8,128)(2,1)}), bf16[16,128,512]{2,1,0:T(8,128)(2,1)}) %all-gather.2.cloned.1.call-update) | async-done | bytes 2097168 | tf_op jit(solution)/shard_map/all_gather | solution.py:272
  53.7 0.0 copy-done.2
  53.7 0.0 copy-done.1
  53.7 3.0 %shard_map.70 = (f32[16,5,8,128]{3,2,1,0:T(8,128)S(1)}, bf16[8,2,128,512]{3,2,1,0:T(8,128)(2,1)S(1)}, bf16[8,64,256]{2,1,0:T(8,128)(2,1)S(1)}) custom-call(s32[32]{0:T(128)S(1)} %reshape.24.tiles, bf16[16,256,128]{2,1,0:T(8,128)(2,1)S(1)} %all-to-all-done.strip, bf16[8,2,128,512]{3,2,1,0:T(8,128)(2,1)} %bitcast.14, f32[1,128]{1,0:T(1,128)S(1)} %copy-done.1, ...), custom_call_target="tpu_custom_call" | custom-call | tf_op jit(solution)/shard_map/pallas_call | solution.py:302
  56.7 20.0 %all_to_all.30.arrived = f32[16,5,8,128]{3,2,1,0:T(8,128)S(1)} all-to-all(f32[16,5,8,128]{3,2,1,0:T(8,128)S(1)} %get-tuple-element.13), channel_id=1, replica_groups=mesh['row'=8,'col'=16,'grid'=2] {'row','grid'}, dimensions={0} | all-to-all | bytes 655360 | tf_op jit(solution)/shard_map/all_to_all | solution.py:286
  76.7 0.1 collective-permute-start.2
  76.8 1.2 collective-permute-done.2.other
  78.0 1.7 shard_map.72
  79.7 19.5 %all_to_all.31.pieces = bf16[16,1,256,128]{3,2,1,0:T(8,128)(2,1)S(1)} all-to-all(bf16[16,1,256,128]{3,2,1,0:T(8,128)(2,1)S(1)} %shard_map.72), channel_id=1, replica_groups=mesh['row'=8,'col'=16,'grid'=2] {'col'}, dimensions={0} | all-to-all | bytes 2097152 | tf_op jit(solution)/shard_map/all_to_all | solution.py:298
  99.1 0.3 shard_map.73
  99.5 18.5 %all_to_all.32.strip = bf16[16,256,128]{2,1,0:T(8,128)(2,1)S(1)} all-to-all(bf16[16,256,128]{2,1,0:T(8,128)(2,1)S(1)} %get-tuple-element.20), channel_id=1, replica_groups=mesh['row'=8,'col'=16,'grid'=2] {'col'}, dimensions={0} | all-to-all | bytes 2097152 | tf_op jit(solution)/shard_map/all_to_all | solution.py:315
  117.9 1.4 shard_map.75
  119.3 17.8 %all_to_all.33.arrived = f32[16,4,8,128]{3,2,1,0:T(8,128)S(1)} all-to-all(f32[16,4,8,128]{3,2,1,0:T(8,128)S(1)} %shard_map.75), channel_id=1, replica_groups=mesh['row'=8,'col'=16,'grid'=2] {'row','grid'}, dimensions={0} | all-to-all | bytes 524288 | tf_op jit(solution)/shard_map/all_to_all | solution.py:286
  137.2 0.1 collective-permute-start.5
  137.3 1.2 collective-permute-done.5.other
  138.4 3.3 %shard_map.77 = bf16[16,2,256,128]{3,2,1,0:T(8,128)(2,1)} custom-call(s32[32]{0:T(128)S(1)} %reshape.24.tiles, f32[4,8,128]{2,1,0:T(8,128)S(1)} %shard_map.76.own, f32[4,8,128]{2,1,0:T(8,128)S(1)} %collective-permute-done.5.other, bf16[8,2,128,512]{3,2,1,0:T(8,128)(2,1)S(1)} %get-tuple-element.15.basis, bf16[8,64,256]{2,1,0:T(8,128)(2,1)S(1)} %get-tuple-element.16.rows), custom_call_target="tpu_custom_call" | custom-call | tf_op jit(solution)/shard_map/pallas_call | solution.py:291
  141.7 3.7 %all-to-all-start.5 = ((bf16[16,2,256,128]{3,2,1,0:T(8,128)(2,1)}), bf16[16,2,256,128]{3,2,1,0:T(8,128)(2,1)S(1)}, u32[]{:S(2)}, u32[]{:S(2)}) async-start(bf16[16,2,256,128]{3,2,1,0:T(8,128)(2,1)} %shard_map.77), calls=%async_computation.5 | async-start | bytes 4194304 | tf_op jit(solution)/shard_map/all_to_all | solution.py:298
  145.4 0.7 collective-permute-start.3
  146.1 0.0 collective-permute-done.3.mine
  146.1 0.3 collective-permute-start.4
  146.4 1.1 collective-permute-done.4.theirs
  147.5 0.7 shard_map.74
  148.2 28.5 %all-to-all-done.5.pieces = bf16[16,2,256,128]{3,2,1,0:T(8,128)(2,1)S(1)} async-done(((bf16[16,2,256,128]{3,2,1,0:T(8,128)(2,1)}), bf16[16,2,256,128]{3,2,1,0:T(8,128)(2,1)S(1)}, u32[]{:S(2)}, u32[]{:S(2)}) %all-to-all-start.5) | async-done | bytes 2097184 | tf_op jit(solution)/shard_map/all_to_all | solution.py:298
  176.7 0.9 shard_map.78
  (2 shorter events, 0.1 us)
Async XLA Ops:
  7.2 25.9 %copy-start.3 = (s32[128,4]{0,1:T(4,128)S(1)}, s32[128,4]{0,1:T(4,128)}, u32[]{:S(2)}) copy-start(s32[128,4]{0,1:T(4,128)} %param.9) | copy-start | bytes 6148
  7.2 46.5 %copy-start.2 = (s32[1,128]{1,0:T(1,128)S(1)}, s32[1,128]{1,0:T(1,128)}, u32[]{:S(2)}) copy-start(s32[1,128]{1,0:T(1,128)} %screen.3) | copy-start | bytes 1540
  7.2 46.5 %copy-start.1 = (f32[1,128]{1,0:T(1,128)S(1)}, f32[1,128]{1,0:T(1,128)}, u32[]{:S(2)}) copy-start(f32[1,128]{1,0:T(1,128)} %weight.3) | copy-start | bytes 1540
  7.2 46.5 %all-gather.2.cloned.1.call-start = ((), (), s32[]{:S(2)}) async-start(), calls=%async_computation.6 | async-start | bytes 2228224 | tf_op jit(solution)/shard_map/all_gather | solution.py:272
  7.9 0.9 copy-start
  9.0 0.7 collective-permute-start
  9.7 4.2 %collective-permute-start.1 = (bf16[2,128,128]{2,1,0:T(8,128)(2,1)S(1)}, bf16[2,128,128]{2,1,0:T(8,128)(2,1)S(1)}, u32[]{:S(2)}, u32[]{:S(2)}) collective-permute-start(bf16[2,128,128]{2,1,0:T(8,128)(2,1)S(1)} %collective-permute-done.mine), channel_id=1, source_target_pairs={{0,1},{1,0},{2,3},{3,2},{4,5},{5,4},{6,7},{7,6},{8,9},{9,8},{10,11... | collective-permute-start | bytes 196616 | tf_op jit(solution)/shard_map/ppermute | solution.py:276
  15.1 33.7 %all-to-all-start = ((bf16[16,256,128]{2,1,0:T(8,128)(2,1)}), bf16[16,256,128]{2,1,0:T(8,128)(2,1)S(1)}, u32[]{:S(2)}, u32[]{:S(2)}) async-start(bf16[16,256,128]{2,1,0:T(8,128)(2,1)} %get-tuple-element.12), calls=%async_computation | async-start | bytes 2097152 | tf_op jit(solution)/shard_map/all_to_all | solution.py:301
  76.7 1.3 collective-permute-start.2
  137.2 1.3 collective-permute-start.5
  141.7 35.0 %all-to-all-start.5 = ((bf16[16,2,256,128]{3,2,1,0:T(8,128)(2,1)}), bf16[16,2,256,128]{3,2,1,0:T(8,128)(2,1)S(1)}, u32[]{:S(2)}, u32[]{:S(2)}) async-start(bf16[16,2,256,128]{3,2,1,0:T(8,128)(2,1)} %shard_map.77), calls=%async_computation.5 | async-start | bytes 4194304 | tf_op jit(solution)/shard_map/all_to_all | solution.py:298
  145.4 0.7 collective-permute-start.3
  146.1 1.3 collective-permute-start.4
Sparse Core Ops, SparseCore 0:
  9.9 43.7 all-gather.1
